TPU v7x, 512 devices: a whole 4x4x16 slice. The times are simulated.
512 devices in a mesh: wide: 64 (over x, z_lo, core), narrow: 8 (over y, z_hi).
Axes of the slice: x: 4, y: 4, z: 16 (z_hi: 2, z_lo: 8; z = z_hi * 8 + z_lo), core: 2. Of those that a mesh axis runs over, the one named last changes fastest.
Arguments:
- surface_prev: float32 [8192, 1024], P('wide', 'narrow'), may hold values from -6 to 6
- surface_now: float32 [8192, 1024], P('wide', 'narrow'), may hold values from -6 to 6
- eastward_prev: float32 [8192, 1024], P('wide', 'narrow'), may hold values from -6 to 6
- eastward_now: float32 [8192, 1024], P('wide', 'narrow'), may hold values from -6 to 6
- northward_prev: float32 [8192, 1024], P('wide', 'narrow'), may hold values from -6 to 6
- northward_now: float32 [8192, 1024], P('wide', 'narrow'), may hold values from -6 to 6
- depth_west: float32 [8192, 1024], P('wide', 'narrow'), may hold values from 0 to 1.2, as said below
- depth_south: float32 [8192, 1024], P('wide', 'narrow'), may hold values from 0 to 1.2, as said below
- edge_links: int32 [8, 4, 3], replicated, may hold values from 0 to 7, as said below
- phase_start: float32 [8], replicated, may hold values from -3.140625 to 3.140625
Outputs:
- surface_last: float32 [8192, 1024], P('wide', 'narrow')
- eastward_last: float32 [8192, 1024], P('wide', 'narrow')
- northward_last: float32 [8192, 1024], P('wide', 'narrow')
- harmonics: float32 [16, 8192, 1024], P(None, 'wide', 'narrow')
Inputs may be any that keep to these rules, and one draw needn't show every extreme that they name: edge_links[f, e] = (g, k, r) says that edge e of face f (0 west, 1 south, 2 east, 3 north) is glued to edge k of face g, with cells in opposite order along the edge when r = 1. The relation is symmetric: edge_links[g, k] = (f, e, r). West and south edges are glued only to east and north edges, and the reverse. `depth_west`: zero at land sides, positive elsewhere. `depth_south`: zero at land sides, positive elsewhere.
All inputs are finite; a program needn't handle non-finite values.
Results may differ from a plain program's by a relative error of at most 0.000071.
Values sent between devices are 32-bit elements; how exact they have to be, the bound alone decides.
A program may use at most 64 MiB of HBM per device.

v0:
```python
import jax
import jax.numpy as jnp
from jax import lax
from jax.sharding import PartitionSpec as P

SUBSTEPS = 4
CONSTITUENTS = 8


tide_omega = (
    0.0001405189,
    0.0001454441,
    0.0001378797,
    0.0001458423,
    7.292117e-05,
    6.759774e-05,
    7.251056e-05,
    6.495854e-05,
)
step_seconds = 25.0
mass_factor = 0.3
flow_factor = 0.3
filter_weight = 0.1


def phase_rows(phase_start):
    counter_values = jnp.arange(1, SUBSTEPS + 1).astype(jnp.float32)
    tide_rates = jnp.array(tide_omega, jnp.float32) * step_seconds
    angles = phase_start[:, None] + tide_rates[:, None] * counter_values[None, :]
    return jnp.concatenate([jnp.cos(angles), jnp.sin(angles)], axis=0)


def pick_line(link_row, first_kind, first_lines, second_lines):
    face_id = link_row[0]
    first_line = lax.dynamic_index_in_dim(first_lines, face_id, 0, keepdims=False)
    second_line = lax.dynamic_index_in_dim(second_lines, face_id, 0, keepdims=False)
    chosen = jnp.where(link_row[1] == first_kind, first_line, second_line)
    return jnp.where(link_row[2] == 1, chosen[::-1], chosen)


def segment(full_line, first_cell, span_cells):
    return lax.dynamic_slice_in_dim(full_line, first_cell, span_cells, 0)


def pick_row(table_rows, position):
    return lax.dynamic_index_in_dim(table_rows, position, 0, keepdims=False)


def body(
    surface_prev,
    surface_now,
    eastward_prev,
    eastward_now,
    northward_prev,
    northward_now,
    depth_west,
    depth_south,
    edge_links,
    phase_start,
):
    row_count, col_count = surface_now.shape
    wide_count = lax.axis_size("wide")
    narrow_count = lax.axis_size("narrow")
    face_side = col_count * narrow_count
    tile_rows = face_side // row_count
    face_count = wide_count // tile_rows
    wide_index = lax.axis_index("wide")
    narrow_index = lax.axis_index("narrow")
    face_id = wide_index // tile_rows
    tile_row = wide_index % tile_rows
    my_links = lax.dynamic_index_in_dim(edge_links, face_id, 0, keepdims=False)
    row_start = tile_row * row_count
    col_start = narrow_index * col_count
    west_at = row_count + col_count
    south_at = 2 * row_count + col_count
    west_index = jnp.maximum(narrow_index - 1, 0)
    east_index = jnp.minimum(narrow_index + 1, narrow_count - 1)
    south_index = jnp.maximum(wide_index - 1, 0)
    north_index = jnp.minimum(wide_index + 1, wide_count - 1)
    snapshots = []
    for substep in range(SUBSTEPS):
        flux_west = depth_west * eastward_now
        flux_south = depth_south * northward_now
        offered = jnp.concatenate(
            [surface_now[:, -1], surface_now[-1, :], flux_west[:, 0], flux_south[0, :]]
        )[None, :]
        row_bundle = lax.all_gather(offered, "narrow", axis=0, tiled=True)
        west_near = pick_row(row_bundle, west_index)[:row_count]
        east_near = pick_row(row_bundle, east_index)[west_at:south_at]
        packed = jnp.concatenate(
            [
                surface_now[-1, :],
                flux_south[0, :],
                row_bundle[-1, :row_count],
                row_bundle[0, west_at:south_at],
                row_bundle[:, row_count:west_at].reshape(face_side),
                row_bundle[:, south_at:].reshape(face_side),
            ]
        )[None, :]
        column = lax.all_gather(packed, "wide", axis=0, tiled=True)
        south_near = pick_row(column, south_index)[:col_count]
        north_near = pick_row(column, north_index)[col_count : 2 * col_count]
        column_grid = column.reshape(face_count, tile_rows, column.shape[1])
        lead_cells = 2 * col_count
        east_lines = column_grid[:, :, lead_cells : lead_cells + row_count].reshape(
            face_count, face_side
        )
        west_lines = column_grid[:, :, lead_cells + row_count : lead_cells + 2 * row_count].reshape(
            face_count, face_side
        )
        north_lines = column_grid[
            :, -1, lead_cells + 2 * row_count : lead_cells + 2 * row_count + face_side
        ]
        south_lines = column_grid[:, 0, lead_cells + 2 * row_count + face_side :]
        west_ghost = jnp.where(
            narrow_index == 0,
            segment(pick_line(my_links[0], 2, east_lines, north_lines), row_start, row_count),
            west_near,
        )
        south_ghost = jnp.where(
            tile_row == 0,
            segment(pick_line(my_links[1], 2, east_lines, north_lines), col_start, col_count),
            south_near,
        )
        east_ghost = jnp.where(
            narrow_index == narrow_count - 1,
            segment(pick_line(my_links[2], 0, west_lines, south_lines), row_start, row_count),
            east_near,
        )
        north_ghost = jnp.where(
            tile_row == tile_rows - 1,
            segment(pick_line(my_links[3], 0, west_lines, south_lines), col_start, col_count),
            north_near,
        )
        flux_east = jnp.concatenate([flux_west[:, 1:], east_ghost[:, None]], axis=1)
        flux_north = jnp.concatenate([flux_south[1:, :], north_ghost[None, :]], axis=0)
        surface_west = jnp.concatenate([west_ghost[:, None], surface_now[:, :-1]], axis=1)
        surface_south = jnp.concatenate([south_ghost[None, :], surface_now[:-1, :]], axis=0)
        divergence = flux_east - flux_west + (flux_north - flux_south)
        surface_next = surface_prev - 2.0 * mass_factor * divergence
        eastward_next = eastward_prev - 2.0 * flow_factor * (surface_now - surface_west)
        northward_next = northward_prev - 2.0 * flow_factor * (surface_now - surface_south)
        surface_prev = surface_now + filter_weight * (
            surface_prev - 2.0 * surface_now + surface_next
        )
        eastward_prev = eastward_now + filter_weight * (
            eastward_prev - 2.0 * eastward_now + eastward_next
        )
        northward_prev = northward_now + filter_weight * (
            northward_prev - 2.0 * northward_now + northward_next
        )
        surface_now = surface_next
        eastward_now = eastward_next
        northward_now = northward_next
        snapshots.append(surface_now)
    stacked = jnp.stack(snapshots).reshape(SUBSTEPS, row_count * col_count)
    harmonics = jnp.dot(phase_rows(phase_start), stacked, precision=lax.Precision.HIGHEST)
    return (
        surface_now,
        eastward_now,
        northward_now,
        harmonics.reshape(2 * CONSTITUENTS, row_count, col_count),
    )


def solution(mesh):
    in_specs = (
        P("wide", "narrow"),
        P("wide", "narrow"),
        P("wide", "narrow"),
        P("wide", "narrow"),
        P("wide", "narrow"),
        P("wide", "narrow"),
        P("wide", "narrow"),
        P("wide", "narrow"),
        P(),
        P(),
    )
    out_specs = (
        P("wide", "narrow"),
        P("wide", "narrow"),
        P("wide", "narrow"),
        P(None, "wide", "narrow"),
    )
    return jax.shard_map(body, mesh=mesh, in_specs=in_specs, out_specs=out_specs, check_vma=False)
```

profile of v0, /device:TPU:1, one launch (start us, length us, event | category | flops | bytes accessed | tf_op | source)
XLA Modules:
  0.0 741.5 jit_solution(16598307626363731102)
XLA Ops:
  0.8 0.5 copy-done.11
  1.5 0.7 fusion.86
  15.0 0.8 copy-done.3
  15.8 0.2 slice_reduce_fusion.6
  16.0 58.5 %all-gather.8 = f32[8,1,512]{2,1,0:T(1,128)S(1)} all-gather(f32[1,1,512]{2,1,0:T(1,128)S(1)} %bitcast.434), channel_id=2, replica_groups=mesh['wide'=64,'narrow'=8] {'narrow'}, dimensions={0}, use_global_device_ids=true | all-gather | bytes 18432 | tf_op jit(solution)/shard_map/all_gather | solution.py:87
  74.6 130.8 %all-gather.9 = f32[64,1,2560]{2,1,0:T(1,128)S(1)} all-gather(f32[1,1,2560]{2,1,0:T(1,128)S(1)} %reshape.216), channel_id=3, replica_groups=mesh['wide'=64,'narrow'=8] {'wide'}, dimensions={0}, use_global_device_ids=true | all-gather | bytes 665600 | tf_op jit(solution)/shard_map/all_gather | solution.py:100
  206.6 0.6 copy-done.1
  207.4 0.2 slice_reduce_fusion.5
  207.5 0.5 copy-done.7
  208.4 53.9 %all-gather.10 = f32[8,1,512]{2,1,0:T(1,128)S(1)} all-gather(f32[1,1,512]{2,1,0:T(1,128)S(1)} %bitcast.435), channel_id=4, replica_groups=mesh['wide'=64,'narrow'=8] {'narrow'}, dimensions={0}, use_global_device_ids=true | all-gather | bytes 18432 | tf_op jit(solution)/shard_map/all_gather | solution.py:87
  262.5 120.2 %all-gather.11 = f32[64,1,2560]{2,1,0:T(1,128)S(1)} all-gather(f32[1,1,2560]{2,1,0:T(1,128)S(1)} %reshape.220), channel_id=5, replica_groups=mesh['wide'=64,'narrow'=8] {'wide'}, dimensions={0}, use_global_device_ids=true | all-gather | bytes 665600 | tf_op jit(solution)/shard_map/all_gather | solution.py:100
  383.7 0.1 copy.35
  383.9 0.2 slice_reduce_fusion.3
  384.1 0.1 copy.36
  384.5 54.0 %all-gather.12 = f32[8,1,512]{2,1,0:T(1,128)S(1)} all-gather(f32[1,1,512]{2,1,0:T(1,128)S(1)} %bitcast.436), channel_id=6, replica_groups=mesh['wide'=64,'narrow'=8] {'narrow'}, dimensions={0}, use_global_device_ids=true | all-gather | bytes 18432 | tf_op jit(solution)/shard_map/all_gather | solution.py:87
  438.6 122.2 %all-gather.13 = f32[64,1,2560]{2,1,0:T(1,128)S(1)} all-gather(f32[1,1,2560]{2,1,0:T(1,128)S(1)} %reshape.224), channel_id=7, replica_groups=mesh['wide'=64,'narrow'=8] {'wide'}, dimensions={0}, use_global_device_ids=true | all-gather | bytes 665600 | tf_op jit(solution)/shard_map/all_gather | solution.py:100
  561.8 0.1 copy.37
  562.0 0.2 slice_reduce_fusion.1
  562.4 53.9 %all-gather.14 = f32[8,1,512]{2,1,0:T(1,128)S(1)} all-gather(f32[1,1,512]{2,1,0:T(1,128)S(1)} %bitcast.437), channel_id=8, replica_groups=mesh['wide'=64,'narrow'=8] {'narrow'}, dimensions={0}, use_global_device_ids=true | all-gather | bytes 18432 | tf_op jit(solution)/shard_map/all_gather | solution.py:87
  616.5 120.3 %all-gather.15 = f32[64,1,2560]{2,1,0:T(1,128)S(1)} all-gather(f32[1,1,2560]{2,1,0:T(1,128)S(1)} %reshape.228), channel_id=9, replica_groups=mesh['wide'=64,'narrow'=8] {'wide'}, dimensions={0}, use_global_device_ids=true | all-gather | bytes 665600 | tf_op jit(solution)/shard_map/all_gather | solution.py:100
  738.0 0.1 copy.40
  738.1 0.8 fusion.34
  738.9 1.3 fusion
  740.2 1.3 copy.41
  (201 shorter events, 5.8 us)
Async XLA Ops:
  0.6 0.7 copy-start.11
  0.7 0.8 copy-start.9
  0.7 14.2 %copy-start.4 = (f32[128,128]{1,0:T(8,128)S(1)}, f32[128,128]{1,0:T(8,128)}, u32[]{:S(2)}) copy-start(f32[128,128]{1,0:T(8,128)} %param.16) | copy-start | bytes 196612
  0.7 0.7 copy-start.10
  0.7 14.1 %copy-start = (f32[128,128]{1,0:T(8,128)S(1)}, f32[128,128]{1,0:T(8,128)}, u32[]{:S(2)}) copy-start(f32[128,128]{1,0:T(8,128)} %param.12) | copy-start | bytes 196612
  0.7 14.2 %copy-start.2 = (f32[128,128]{1,0:T(8,128)S(1)}, f32[128,128]{1,0:T(8,128)}, u32[]{:S(2)}) copy-start(f32[128,128]{1,0:T(8,128)} %param.18) | copy-start | bytes 196612
  14.9 0.8 copy-start.3
  14.9 0.9 copy-start.5
  206.4 0.8 copy-start.1
  207.2 0.8 copy-start.7
  207.3 0.8 copy-start.6
  738.0 0.9 copy-start.8
where the time goes:
time: 742 us; the launch traced here: 741 us
  blocking collectives  714 us (96%)
  between operations  14.2 us (2%)
  local copies, waits for them, and re-layouts  9.09 us (1%)
    all_gather x4, blocking collectives, body(): column = lax.all_gather(packed, 'wide', axis=0, tiled=True)  494 us
    all_gather x4, blocking collectives, body(): row_bundle = lax.all_gather(offered, 'narrow', axis=0, tiled=True)  220 us

commit v1 on v0

v1 whole, which is shorter than its diff:
```python
import functools

import jax
import jax.numpy as jnp
from jax import lax
from jax.experimental import pallas as pl
from jax.experimental.pallas import tpu as pltpu
from jax.sharding import PartitionSpec as P

MESH = pl.DeviceIdType.MESH
SUBSTEPS = 4
CONSTITUENTS = 8
tide_omega = (
    0.0001405189,
    0.0001454441,
    0.0001378797,
    0.0001458423,
    7.292117e-05,
    6.759774e-05,
    7.251056e-05,
    6.495854e-05,
)
step_seconds = 25.0
G = 0.6
W, S, E, N = range(4)
LINES = 9


def rims(s, sp, n, np_, t, tp, dn, dt):
    last = s.shape[0] - 1
    row = lambda x, i: x[i : i + 1, :]
    a, b = last, last - 1
    n1 = row(np_, a) - G * (row(s, a) - row(s, b))
    fa = row(dn, a) * row(n, a)
    fb = row(dn, b) * row(n, b)
    back = G * row(dn, a)
    older = 0.8 * row(n, a) + 0.1 * row(np_, a) + 0.1 * n1
    high = [
        row(s, a),
        row(sp, a) + G * fa,
        0.8 * row(s, a) + 0.1 * row(sp, a) + G * (row(dn, a) * n1),
        0.08 * row(s, a)
        + 0.01 * row(sp, a)
        + G * (row(dn, a) * older + back * (row(sp, b) - G * (fa - fb))),
        back,
        row(dt, a) * row(t, a),
        row(dt, a) * row(tp, a),
        G * row(dt, a),
        row(dt, b) * row(t, b),
    ]
    a, b = 0, 1
    n1 = row(np_, b) - G * (row(s, b) - row(s, a))
    fa = row(dn, a) * row(n, a)
    fb = row(dn, b) * row(n, b)
    low = [
        row(s, a),
        row(sp, a) - G * (fb - fa),
        0.8 * row(s, a) + 0.1 * row(sp, a) - G * (row(dn, b) * n1),
        row(dn, a) * row(np_, a),
        G * row(dn, a),
        row(dt, a) * row(t, a),
        row(dt, a) * row(tp, a),
        G * row(dt, a),
        fa,
    ]
    return low, high


def exchange(
    sides, faces, ph, sp, s, up, u, vp, v, dw, ds,
    ws_ref, en_ref, wx_ref, ex_ref, cx_ref, dx_ref, coef_ref,
    pack, ends,
    near_send, near_recv, diag_send, diag_recv, main_send, ext_send, ws_recv, en_recv, wx_recv, ex_recv, own_sem, corner_send, corner_recv,
):
    last = sides - 1
    w = lax.axis_index("wide")
    c = lax.axis_index("narrow")
    f = w // sides
    r = w % sides
    at = lambda face, row, col: (face * sides + row, col)
    signal = lambda bar, d: pl.semaphore_signal(bar, inc=1, device_id=d, device_id_type=MESH)
    is_end = lambda q: (q == 0) | (q == last)
    corner = is_end(r) & is_end(c)
    has_ws = (c == 0) | (r == 0)
    has_en = (c == last) | (r == last)
    seg_ws = jnp.where(c == 0, r, c)
    seg_en = jnp.where(c == last, r, c)
    corner_at = lambda i: at(i // 4, (i // 2) % 2 * last, i % 2 * last)
    me_corner = f * 4 + (r // last) * 2 + c // last

    bar = pltpu.get_barrier_semaphore()
    around = [
        (dr, dc, (r + dr >= 0) & (r + dr <= last) & (c + dc >= 0) & (c + dc <= last))
        for dr in (-1, 0, 1)
        for dc in (-1, 0, 1)
        if (dr, dc) != (0, 0)
    ]
    awaited = jnp.int32(0)
    for dr, dc, there in around:
        awaited += there.astype(jnp.int32)

        @pl.when(there)
        def _(dr=dr, dc=dc):
            signal(bar, at(f, r + dr, c + dc))

    def greet(seg, line):
        def body(g, _):
            for q in (seg, last - seg):
                for row, col in ((q, line), (line, q)):

                    @pl.when(~((g == f) & (row == r) & (col == c)))
                    def _(row=row, col=col):
                        signal(bar, at(g, row, col))

            for q in (seg - 1, seg + 1, last - 1 - seg, last + 1 - seg):

                @pl.when((q >= 0) & (q <= last))
                def _(q=q):
                    signal(bar, at(g, q, line))
                    signal(bar, at(g, line, q))

            return 0

        lax.fori_loop(0, faces, body, 0)

    @pl.when(has_ws)
    def _():
        greet(seg_ws, last)

    @pl.when(has_en)
    def _():
        greet(seg_en, 0)

    @pl.when(corner)
    def _():
        def body(i, _):
            @pl.when(i != me_corner)
            def _():
                signal(bar, corner_at(i))

            return 0

        lax.fori_loop(0, 4 * faces, body, 0)

    lo, hi = rims(s[...], sp[...], v[...], vp[...], u[...], up[...], ds[...], dw[...])
    for k in range(LINES):
        pack[S, k : k + 1, :] = lo[k]
        pack[N, k : k + 1, :] = hi[k]
    flip = lambda x: jnp.transpose(x[...])
    lo, hi = rims(flip(s), flip(sp), flip(u), flip(up), flip(v), flip(vp), flip(dw), flip(ds))
    for k in range(LINES):
        pack[W, k : k + 1, :] = lo[k]
        pack[E, k : k + 1, :] = hi[k]
    side = s.shape[0]
    for e in range(4):
        pack[e, LINES:16, :] = jnp.zeros((16 - LINES, side), jnp.float32)
    stacked = jnp.concatenate([pack[e] for e in range(4)] + [jnp.zeros((side - 64, side), jnp.float32)], axis=0)
    turned = jnp.transpose(stacked)
    lane = lax.broadcasted_iota(jnp.int32, (1, side), 1)
    for e in range(4):
        gathered = jnp.zeros((1, side), jnp.float32)
        for k, i in enumerate((0, 1, side - 2, side - 1)):
            moved = turned[i : i + 1, :]
            by = (16 * k - 16 * e) % side
            if by:
                moved = pltpu.roll(moved, by, 1)
            gathered = jnp.where((lane >= 16 * k) & (lane < 16 * k + 16), moved, gathered)
        ends[e] = gathered

    which = lax.broadcasted_iota(jnp.int32, (CONSTITUENTS, side), 0)
    count = (lax.broadcasted_iota(jnp.int32, (CONSTITUENTS, side), 1) + 1).astype(jnp.float32)
    start = jnp.zeros((CONSTITUENTS, side), jnp.float32)
    rate = jnp.zeros((CONSTITUENTS, side), jnp.float32)
    for k in range(CONSTITUENTS):
        start = jnp.where(which == k, ph[k], start)
        rate = jnp.where(which == k, jnp.float32(tide_omega[k]) * jnp.float32(step_seconds), rate)
    angle = start + rate * count
    coef_ref[0:CONSTITUENTS, :] = jnp.cos(angle)
    coef_ref[CONSTITUENTS:, :] = jnp.sin(angle)

    edges = [
        (E, 0, True, c == last, r, r == 0),
        (N, 1, True, r == last, c, c == 0),
        (W, 0, False, c == 0, r, r == last),
        (S, 1, False, r == 0, c, c == last),
    ]
    n_main = lambda q, own: jnp.where(is_end(q), 3 * faces - own.astype(jnp.int32), 4 * faces)
    n_ext = lambda q: jnp.where(is_end(q), 4 * faces, jnp.where((q == 1) | (q == last - 1), 7 * faces, 8 * faces))
    for _, _, _, has, q, own in edges:
        awaited += jnp.where(has, n_main(q, own) + n_ext(q), 0)
    awaited += jnp.where(corner, 4 * faces - 1, 0)
    pl.semaphore_wait(bar, awaited)

    block = pl.ds(0, LINES)
    for e, kind, to_ws, has, q, own in edges:
        dst, dst_x = (ws_ref, wx_ref) if to_ws else (en_ref, ex_ref)
        got, got_x = (ws_recv, wx_recv) if to_ws else (en_recv, ex_recv)
        line = 0 if to_ws else last

        @pl.when(has)
        def _(e=e, kind=kind, q=q, own=own, dst=dst, dst_x=dst_x, got=got, got_x=got_x, line=line):
            def send_main(g, _):
                for par in range(2):
                    to = q if par == 0 else last - q
                    slot = (f * 2 + kind) * 2 + par
                    for k, (row, col) in enumerate(((to, line), (line, to))):
                        mine = (g == f) & (row == r) & (col == c)
                        once = ~mine if k == 0 else ~mine & (to != line)

                        @pl.when(once)
                        def _(slot=slot, row=row, col=col):
                            pltpu.make_async_remote_copy(
                                pack.at[e, block], dst.at[slot, block], main_send.at[e], got.at[0],
                                device_id=at(g, row, col), device_id_type=MESH,
                            ).start()

                        if k == 0:
                            local = mine
                        else:
                            local = mine & (to != line)

                        @pl.when(local)
                        def _(slot=slot):
                            pltpu.make_async_copy(pack.at[e, block], dst.at[slot, block], got.at[0]).start()

                return 0

            lax.fori_loop(0, faces, send_main, 0)

            def send_ext(g, _):
                for kind_x, to in enumerate((q + 1, q - 1, last - 1 - q, last + 1 - q)):
                    slot = (f * 2 + kind) * 4 + kind_x
                    there = (to >= 0) & (to <= last)
                    for k, (row, col) in enumerate(((to, line), (line, to))):

                        @pl.when(there if k == 0 else there & (to != line))
                        def _(slot=slot, row=row, col=col):
                            pltpu.make_async_remote_copy(
                                ends.at[e], dst_x.at[slot], ext_send.at[e], got_x.at[0],
                                device_id=at(g, row, col), device_id_type=MESH,
                            ).start()

                return 0

            lax.fori_loop(0, faces, send_ext, 0)

    @pl.when(corner)
    def _():
        def body(i, _):
            @pl.when(i != me_corner)
            def _():
                pltpu.make_async_remote_copy(
                    ends, cx_ref.at[me_corner], corner_send.at[0], corner_recv.at[0], device_id=corner_at(i), device_id_type=MESH
                ).start()

            @pl.when(i == me_corner)
            def _():
                pltpu.make_async_copy(ends, cx_ref.at[me_corner], corner_recv.at[0]).start()

            return 0

        lax.fori_loop(0, 4 * faces, body, 0)

    near = [
        (E, ws_ref, 4 * faces, 0, 1),
        (N, ws_ref, 4 * faces + 1, 1, 0),
        (W, en_ref, 4 * faces, 0, -1),
        (S, en_ref, 4 * faces + 1, -1, 0),
    ]
    diagonal = [(0, 1, 1), (1, 1, -1), (2, -1, 1), (3, -1, -1)]
    inside = lambda row, col: (row >= 0) & (row <= last) & (col >= 0) & (col <= last)
    for e, dst, slot, dr, dc in near:

        @pl.when(inside(r + dr, c + dc))
        def _(e=e, dst=dst, slot=slot, dr=dr, dc=dc):
            pltpu.make_async_remote_copy(
                pack.at[e, block], dst.at[slot, block], near_send.at[e], near_recv.at[e],
                device_id=at(f, r + dr, c + dc), device_id_type=MESH,
            ).start()

    for k, dr, dc in diagonal:

        @pl.when(inside(r + dr, c + dc))
        def _(k=k, dr=dr, dc=dc):
            pltpu.make_async_remote_copy(
                ends, dx_ref.at[k], diag_send.at[k], diag_recv.at[k], device_id=at(f, r + dr, c + dc), device_id_type=MESH
            ).start()

    here = (w, c)
    take = lambda ref, ss, rs: pltpu.make_async_remote_copy(ref, ref, ss, rs, device_id=here, device_id_type=MESH)
    for e, dst, slot, dr, dc in near:

        @pl.when(inside(r - dr, c - dc))
        def _(e=e, dst=dst, slot=slot):
            take(dst.at[slot, block], near_send.at[e], near_recv.at[e]).wait_recv()

    for k, dr, dc in diagonal:

        @pl.when(inside(r - dr, c - dc))
        def _(k=k):
            take(dx_ref.at[k], diag_send.at[k], diag_recv.at[k]).wait_recv()

    for has, seg, main, ext, got, got_x in (
        (has_ws, seg_ws, ws_ref, wx_ref, ws_recv, wx_recv),
        (has_en, seg_en, en_ref, ex_ref, en_recv, ex_recv),
    ):

        @pl.when(has)
        def _(seg=seg, main=main, ext=ext, got=got, got_x=got_x):
            take(main.at[pl.ds(0, 4 * faces), block], main_send.at[0], got.at[0]).wait_recv()

            @pl.when(is_end(seg))
            def _():
                take(ext.at[pl.ds(0, 4 * faces)], ext_send.at[0], got_x.at[0]).wait_recv()

            @pl.when(~is_end(seg))
            def _():
                take(ext, ext_send.at[0], got_x.at[0]).wait_recv()

    @pl.when(corner)
    def _():
        take(cx_ref, corner_send.at[0], corner_recv.at[0]).wait_recv()

    for e, dst, slot, dr, dc in near:

        @pl.when(inside(r + dr, c + dc))
        def _(e=e):
            take(pack.at[e, block], near_send.at[e], near_recv.at[e]).wait_send()

    for k, dr, dc in diagonal:

        @pl.when(inside(r + dr, c + dc))
        def _(k=k):
            take(ends, diag_send.at[k], diag_recv.at[k]).wait_send()

    for e, kind, to_ws, has, q, own in edges:
        for n in (3 * faces - 1, 3 * faces, 4 * faces):

            @pl.when(has & (n_main(q, own) == n))
            def _(e=e, n=n):
                take(ws_ref.at[pl.ds(0, n), block], main_send.at[e], ws_recv.at[0]).wait_send()

        for n in (4 * faces, 7 * faces, 8 * faces):

            @pl.when(has & (n_ext(q) == n))
            def _(e=e, n=n):
                take(wx_ref.at[pl.ds(0, n)], ext_send.at[e], wx_recv.at[0]).wait_send()

    @pl.when(corner)
    def _():
        take(cx_ref.at[pl.ds(0, 4 * faces - 1)], corner_send.at[0], corner_recv.at[0]).wait_send()


def substeps(
    sides, faces, links, sp, s, up, u, vp, v, dw, ds, ws, en, wx, ex, cx, dx, coef, s_out, u_out, v_out, h_out,
):
    last = sides - 1
    side = s.shape[0]
    w = lax.axis_index("wide")
    c = lax.axis_index("narrow")
    f = w // sides
    r = w % sides
    lane = lax.broadcasted_iota(jnp.int32, (1, side), 1)
    rows = lax.broadcasted_iota(jnp.int32, (side, side), 0)
    cols = lax.broadcasted_iota(jnp.int32, (side, side), 1)
    mirror = (rows + cols == side - 1).astype(jnp.float32)
    diagonal = rows == cols
    pick = lambda cond, a, b: jnp.where(cond, a, b)
    up_by = lambda x, fill: jnp.where(lane == side - 1, fill, pltpu.roll(x, side - 1, 1))
    down_by = lambda x, fill: jnp.where(lane == 0, fill, pltpu.roll(x, 1, 1))
    head = lambda x: x[:, 0:1]
    tail = lambda x: x[:, side - 1 : side]

    def end(x, k, line):
        return x[:, 16 * k + line : 16 * k + line + 1]

    def corner_of(face, edge, high):
        row = jnp.where(edge == S, 0, jnp.where(edge == N, 1, high))
        col = jnp.where(edge == W, 0, jnp.where(edge == E, 1, high))
        return cx[face * 4 + row * 2 + col, edge]

    def at_end(x, high, k, line):
        return pick(high == 1, end(x, 3 - k, line), end(x, k, line))

    def beyond(face, edge, high):
        far, far_edge, turn = links[face, edge, 0], links[face, edge, 1], links[face, edge, 2]
        stop = high ^ turn
        return at_end(corner_of(far, far_edge, stop), stop, 0, 8)

    def at_corner(face, edge, low_end, inner):
        vertical = (edge == W) | (edge == E)
        side_edge = jnp.where(vertical, S, W) if low_end else jnp.where(vertical, N, E)
        start = (edge >= E).astype(jnp.int32)
        far, far_edge, turn = links[face, side_edge, 0], links[face, side_edge, 1], links[face, side_edge, 2]
        high = start ^ turn
        x = corner_of(far, far_edge, high)
        far_vertical = (far_edge == W) | (far_edge == E)
        third = beyond(far, jnp.where(far_vertical, N, E), (far_edge >= E).astype(jnp.int32))
        ahead = pick(high == 1, third, end(x, 1, 5))
        s1 = at_end(x, high, 0, 1) - G * (ahead - at_end(x, high, 0, 5))
        got = dict(s0=at_end(x, high, 0, 0), s1=s1)
        if low_end:
            got["s1"] = s1 - G * inner
        else:
            got.update(
                T0=at_end(x, high, 0, 8),
                Q=at_end(x, high, 0, 3),
                D=at_end(x, high, 0, 4),
                Tb=at_end(x, high, 1, 8),
            )
        return got

    def ghost(edge, to_ws):
        main, ext = (ws, wx) if to_ws else (en, ex)
        on_face = {W: c == 0, S: r == 0, E: c == last, N: r == last}[edge]
        across = edge in (W, E)
        seg = r if across else c
        face, partner, turn = links[f, edge, 0], links[f, edge, 1], links[f, edge, 2]
        flipped = on_face & (turn == 1)
        kind = (partner == (N if to_ws else S)).astype(jnp.int32)
        q = jnp.where(turn == 1, last - seg, seg)
        slot = jnp.where(on_face, (face * 2 + kind) * 2 + turn, 4 * faces + (0 if across else 1))
        block = main[slot]
        line = [block[k : k + 1, :] for k in range(LINES)]
        slot_x = jnp.where(on_face, (face * 2 + kind) * 4 + 2 * turn, 0)
        strip = (edge + 2) % 4
        lo_at, hi_at = {W: (0, 2), S: (0, 1), E: (1, 3), N: (2, 3)}[edge]
        lo_x = pick(on_face, wx_row(ext, slot_x), dx[lo_at, strip])
        hi_x = pick(on_face, wx_row(ext, slot_x + 1), dx[hi_at, strip])
        first = head(line[5])
        lo = dict(
            s0=end(lo_x, 3, 0), s1=end(lo_x, 3, 1) - G * (first - end(lo_x, 3, 5)),
            F=end(lo_x, 3, 8), R=end(lo_x, 3, 3), Dn=end(lo_x, 3, 4), Fb=end(lo_x, 2, 8),
        )
        hi = dict(
            s0=end(hi_x, 0, 0), s1=end(hi_x, 0, 1) - G * (end(hi_x, 1, 5) - end(hi_x, 0, 5)),
            T0=end(hi_x, 0, 5), Q=end(hi_x, 0, 6), D=end(hi_x, 0, 7), Tb=end(hi_x, 0, 8),
            F=end(hi_x, 0, 8), R=end(hi_x, 0, 3), Dn=end(hi_x, 0, 4), Fb=end(hi_x, 1, 8),
        )
        lo_corner = on_face & (q == 0)
        hi_corner = on_face & (q == last)
        safe = lambda x, top: jnp.where(on_face, x, top)
        g_face, g_edge = safe(face, 0), safe(partner, E if to_ws else W)
        third_lo = at_corner(g_face, g_edge, True, first)
        third_hi = at_corner(g_face, g_edge, False, first)
        for name, value in third_lo.items():
            lo[name] = pick(lo_corner, value, lo[name])
        for name, value in third_hi.items():
            hi[name] = pick(hi_corner, value, hi[name])
        lo["done"], hi["done"] = lo_corner, hi_corner
        turned = jnp.dot(block, mirror, precision=lax.Precision.HIGHEST, preferred_element_type=jnp.float32)
        turned = [turned[k : k + 1, :] for k in range(LINES)]
        along = {5: ("T0", -1.0), 6: ("Q", -1.0), 7: ("D", 1.0)}
        if to_ws:
            along[8] = ("Tb", -1.0)
        out = []
        for k in range(LINES):
            if k in along:
                name, sign = along[k]
                other = sign * down_by(turned[k], hi[name])
            else:
                other = turned[k]
            out.append(pick(flipped, other, line[k]))
        new_lo = {n: pick(flipped, hi[n], lo[n]) for n in ("s0", "s1", "F", "R", "Dn", "Fb")}
        new_hi = {n: pick(flipped, lo[n], hi[n]) for n in ("s0", "s1", "F", "R", "Dn", "Fb")}
        for k, (name, sign) in along.items():
            new_hi[name] = pick(flipped, sign * head(line[k]), hi[name])
        new_lo["done"] = jnp.where(flipped, hi_corner, lo_corner)
        new_hi["done"] = jnp.where(flipped, lo_corner, hi_corner)
        return out, new_lo, new_hi

    def wx_row(ext, slot):
        return ext[slot]

    (wl, w_lo, w_hi), (sl, s_lo, s_hi) = ghost(W, True), ghost(S, True)
    (el, e_lo, e_hi), (nl, n_lo, n_hi) = ghost(E, False), ghost(N, False)

    for d, x in ((w_lo, sl), (w_hi, nl), (s_lo, wl), (s_hi, el)):
        d["s1"] = pick(d["done"], d["s1"], d["s1"] - G * head(x[5]))

    west, south, east, north = c == 0, r == 0, c == last, r == last
    take_w, take_s = west & ~south, south & ~west
    sw_w = {n: pick(take_s, s_lo[n], w_lo[n]) for n in ("s0", "s1")}
    sw_s = {n: pick(take_w, w_lo[n], s_lo[n]) for n in ("s0", "s1")}
    w_lo.update(sw_w)
    s_lo.update(sw_s)
    share = (("s0", "s0"), ("s1", "s1"), ("T0", "F"), ("Q", "R"), ("D", "Dn"), ("Tb", "Fb"))
    take_e, take_s = east & ~south, south & ~east
    se_s = {a: pick(take_e, e_lo[b], s_hi[a]) for a, b in share}
    e_lo["s0"] = pick(take_s, s_hi["s0"], e_lo["s0"])
    s_hi.update(se_s)
    take_n, take_w = north & ~west, west & ~north
    nw_w = {a: pick(take_n, n_lo[b], w_hi[a]) for a, b in share}
    n_lo["s0"] = pick(take_w, w_hi["s0"], n_lo["s0"])
    w_hi.update(nw_w)
    take_e, take_n = east & ~north, north & ~east
    share = (("s0", "s0"), ("T0", "F"), ("Q", "R"), ("D", "Dn"))
    ne_n = {a: pick(take_e, e_hi[b], n_hi[a]) for a, b in share}
    ne_e = {a: pick(take_n, n_hi[b], e_hi[a]) for a, b in share}
    n_hi.update(ne_n)
    e_hi.update(ne_e)

    class HeightRim:
        def __init__(self, line, lo, hi):
            self.line, self.lo, self.hi = line, lo, hi

        def at(self, n, flux):
            s0, y1, y2, z, back, t0, q, d, tb = self.line
            lo, hi = self.lo, self.hi
            if n == 0:
                return s0
            if n == 1:
                self.s1 = y1 - G * flux - G * (up_by(t0, hi["T0"]) - t0)
                return self.s1
            if n == 2:
                self.t1 = q - d * (s0 - down_by(s0, lo["s0"]))
                self.t1hi = hi["Q"] - hi["D"] * (hi["s0"] - tail(s0))
                self.s2 = y2 + 0.1 * self.s1 - G * flux - G * (up_by(self.t1, self.t1hi) - self.t1)
                return self.s2
            s1 = self.s1
            t2 = 0.8 * t0 + 0.1 * q + 0.1 * self.t1 - d * (s1 - down_by(s1, lo["s1"]))
            t2hi = 0.8 * hi["T0"] + 0.1 * hi["Q"] + 0.1 * self.t1hi - hi["D"] * (hi["s1"] - tail(s1))
            inner = s1 + G * (up_by(tb, hi["Tb"]) - tb)
            return 0.81 * s1 + 0.1 * self.s2 + z - G * back * inner - G * flux - G * (up_by(t2, t2hi) - t2)

    class FluxRim:
        def __init__(self, line, lo, hi):
            self.line, self.lo, self.hi = line, lo, hi

        def at(self, n, height):
            s0, u1, u2, r_, d_, t0, q, d, f0 = self.line
            lo, hi = self.lo, self.hi
            if n == 0:
                return f0
            if n == 1:
                self.f1 = r_ - d_ * (s0 - height)
                return self.f1
            if n == 2:
                self.s1 = u1 - G * (up_by(t0, hi["T0"]) - t0)
                self.older = 0.8 * f0 + 0.1 * r_ + 0.1 * self.f1
                self.f2 = self.older - d_ * (self.s1 - height)
                return self.f2
            t1 = q - d * (s0 - down_by(s0, lo["s0"]))
            t1hi = hi["Q"] - hi["D"] * (hi["s0"] - tail(s0))
            s2 = u2 + 0.1 * self.s1 + G * self.f1 - G * (up_by(t1, t1hi) - t1)
            return 0.8 * self.f1 + 0.1 * self.f2 + 0.1 * self.older - d_ * (s2 - height)

    rim_w, rim_s = HeightRim(wl, w_lo, w_hi), HeightRim(sl, s_lo, s_hi)
    rim_e, rim_n = FluxRim(el, e_lo, e_hi), FluxRim(nl, n_lo, n_hi)
    as_row = lambda col: jnp.sum(jnp.where(diagonal, col, 0.0), axis=0, keepdims=True)
    as_col = lambda row: jnp.sum(jnp.where(diagonal, row, 0.0), axis=1, keepdims=True)
    s_, u_, v_ = s[...], u[...], v[...]
    sp_, up_, vp_ = sp[...], up[...], vp[...]
    dw_, ds_ = dw[...], ds[...]
    first_col, last_col = cols == 0, cols == side - 1
    first_row, last_row = rows == 0, rows == side - 1
    flux_w = flux_s = height_e = height_n = None
    snaps = []
    for n in range(SUBSTEPS):
        fw, fs = dw_ * u_, ds_ * v_
        west_line, south_line = rim_w.at(n, flux_w), rim_s.at(n, flux_s)
        east_line, north_line = rim_e.at(n, height_e), rim_n.at(n, height_n)
        flux_w, flux_s = as_row(fw[:, 0:1]), fs[0:1, :]
        height_e, height_n = as_row(s_[:, side - 1 : side]), s_[side - 1 : side, :]
        fe = jnp.where(last_col, as_col(east_line), pltpu.roll(fw, side - 1, 1))
        fn = jnp.where(last_row, north_line, pltpu.roll(fs, side - 1, 0))
        sw = jnp.where(first_col, as_col(west_line), pltpu.roll(s_, 1, 1))
        ss = jnp.where(first_row, south_line, pltpu.roll(s_, 1, 0))
        s_next = sp_ - G * ((fe - fw) + (fn - fs))
        u_next = up_ - G * (s_ - sw)
        v_next = vp_ - G * (s_ - ss)
        sp_ = s_ + 0.1 * (sp_ - 2.0 * s_ + s_next)
        up_ = u_ + 0.1 * (up_ - 2.0 * u_ + u_next)
        vp_ = v_ + 0.1 * (vp_ - 2.0 * v_ + v_next)
        s_, u_, v_ = s_next, u_next, v_next
        snaps.append(s_)
    s_out[...] = s_
    u_out[...] = u_
    v_out[...] = v_
    for k in range(2 * CONSTITUENTS):
        total = coef[k : k + 1, 0:1] * snaps[0]
        for n in range(1, SUBSTEPS):
            total += coef[k : k + 1, n : n + 1] * snaps[n]
        h_out[k] = total


def solution(mesh):
    def body(sp, s, up, u, vp, v, dw, ds, links, ph):
        side = s.shape[0]
        sides = mesh.shape["narrow"]
        faces = mesh.shape["wide"] // sides
        f32 = jnp.float32
        shape = lambda *dims: jax.ShapeDtypeStruct(dims, f32)
        vmem = pl.BlockSpec(memory_space=pltpu.VMEM)
        smem = pl.BlockSpec(memory_space=pltpu.SMEM)
        dma = pltpu.SemaphoreType.DMA
        got = pl.pallas_call(
            functools.partial(exchange, sides, faces),
            out_shape=(
                shape(4 * faces + 2, 16, side),
                shape(4 * faces + 2, 16, side),
                shape(8 * faces, 1, side),
                shape(8 * faces, 1, side),
                shape(4 * faces, 4, 1, side),
                shape(4, 4, 1, side),
                shape(2 * CONSTITUENTS, side),
            ),
            in_specs=[smem] + [vmem] * 8,
            out_specs=(vmem,) * 7,
            scratch_shapes=[
                pltpu.VMEM((4, 16, side), f32),
                pltpu.VMEM((4, 1, side), f32),
                dma((4,)), dma((4,)), dma((4,)), dma((4,)), dma((4,)), dma((4,)),
                dma((1,)), dma((1,)), dma((1,)), dma((1,)), dma((1,)), dma((1,)), dma((1,)),
            ],
            compiler_params=pltpu.CompilerParams(collective_id=0, has_side_effects=True),
        )(ph, sp, s, up, u, vp, v, dw, ds)
        tile = shape(side, side)
        return pl.pallas_call(
            functools.partial(substeps, sides, faces),
            out_shape=(tile, tile, tile, shape(2 * CONSTITUENTS, side, side)),
            in_specs=[smem] + [vmem] * 15,
            out_specs=(vmem,) * 4,
        )(links, sp, s, up, u, vp, v, dw, ds, *got)

    tiles = P("wide", "narrow")
    return jax.shard_map(
        body,
        mesh=mesh,
        in_specs=(tiles,) * 8 + (P(), P()),
        out_specs=(tiles, tiles, tiles, P(None, "wide", "narrow")),
        check_vma=False,
    )
```

time: 742 us -> 47.1 us (0.06)
  blocking collectives: 714 us -> 0 us
  Pallas kernels: 0 us -> 44.8 us
  between operations: 14.2 us -> 0.64 us
  local copies, waits for them, and re-layouts: 9.09 us -> 1.39 us
    all_gather x8 -> x0, blocking collectives: 714 us -> none  [the longest x4 494 us: body(): column = lax.all_gather(packed, 'wide', axis=0, tiled=True)]
    pallas_call x0 -> x2, Pallas kernels: none -> 44.8 us  [the longest x1 40.2 us: body(): pl.pallas_call(functools.partial(exchange, sides, faces), out_shape=(shap...]
where the time goes in v1:
time: 47.1 us; the launch traced here: 46.8 us
  Pallas kernels  44.8 us (95%)
  local copies, waits for them, and re-layouts  1.39 us (3%)
  between operations  0.64 us (1%)
    pallas_call x1, Pallas kernels, body(): pl.pallas_call(functools.partial(exchange, sides, faces), out_shape=(shap...  40.2 us
    pallas_call x1, Pallas kernels, body(): pl.pallas_call(functools.partial(substeps, sides, faces), out_shape=(tile...  4.59 us
    unnamed x1, local copies, waits for them, and re-layouts  1.39 us

profile of v1, /device:TPU:1, one launch (start us, length us, event | category | flops | bytes accessed | tf_op | source)
XLA Modules:
  0.0 46.8 jit_solution(7793942456054584359)
XLA Ops:
  0.6 1.4 %copy.14.links = s32[8,4,3]{2,1,0:T(4,128)} copy(s32[8,4,3]{0,1,2:T(4,128)} %param.18) | data formatting | bytes 768 | tf_op args[8]
  2.0 40.2 %shard_map.129 = (f32[34,16,128]{2,1,0:T(8,128)}, f32[34,16,128]{2,1,0:T(8,128)}, f32[64,1,128]{2,1,0:T(1,128)}, f32[64,1,128]{2,1,0:T(1,128)}, f32[32,4,1,128]{...) custom-call(f32[8]{0:T(128)} %ph.1, f32[128,128]{1,0:T(8,128)} %sp.3, f32[128,128]{1,0:T(8,128)} %s.3, ...), custom_call_target="tpu_custom_call" | custom-call | tf_op jit(solution)/shard_map/pallas_call | solution.py:597
  42.2 4.6 %shard_map.130 = (f32[128,128]{1,0:T(8,128)}, f32[128,128]{1,0:T(8,128)}, f32[128,128]{1,0:T(8,128)}, f32[16,128,128]{2,1,0:T(8,128)}) custom-call(s32[8,4,3]{2,1,0:T(4,128)} %copy.14.links, f32[128,128]{1,0:T(8,128)} %sp.3, f32[128,128]{1,0:T(8,128)} %s.3, f32[128,128]{1,0:T(8,128)} %up.3, f32[128,128]{1,0:T(8,128)} %u.3, f32[128,128]{1,0:T(8,128)} %vp.3, ...), custom_call_target="tpu_custom_call" | custom-call | tf_op jit(solution)/shard_map/pallas_call | solution.py:619

commit v2 on v1

v2 whole, which is shorter than its diff:
```python
import functools

import jax
import jax.numpy as jnp
from jax import lax
from jax.experimental import pallas as pl
from jax.experimental.pallas import tpu as pltpu
from jax.sharding import PartitionSpec as P

MESH = pl.DeviceIdType.MESH
SUBSTEPS = 4
CONSTITUENTS = 8
tide_omega = (
    0.0001405189,
    0.0001454441,
    0.0001378797,
    0.0001458423,
    7.292117e-05,
    6.759774e-05,
    7.251056e-05,
    6.495854e-05,
)
step_seconds = 25.0
G = 0.6
W, S, E, N = range(4)
LINES = 9


def rims(s, sp, n, np_, t, tp, dn, dt):
    last = s.shape[0] - 1
    row = lambda x, i: x[i : i + 1, :]
    a, b = last, last - 1
    n1 = row(np_, a) - G * (row(s, a) - row(s, b))
    fa = row(dn, a) * row(n, a)
    fb = row(dn, b) * row(n, b)
    back = G * row(dn, a)
    older = 0.8 * row(n, a) + 0.1 * row(np_, a) + 0.1 * n1
    high = [
        row(s, a),
        row(sp, a) + G * fa,
        0.8 * row(s, a) + 0.1 * row(sp, a) + G * (row(dn, a) * n1),
        0.08 * row(s, a)
        + 0.01 * row(sp, a)
        + G * (row(dn, a) * older + back * (row(sp, b) - G * (fa - fb))),
        back,
        row(dt, a) * row(t, a),
        row(dt, a) * row(tp, a),
        G * row(dt, a),
        row(dt, b) * row(t, b),
    ]
    a, b = 0, 1
    n1 = row(np_, b) - G * (row(s, b) - row(s, a))
    fa = row(dn, a) * row(n, a)
    fb = row(dn, b) * row(n, b)
    low = [
        row(s, a),
        row(sp, a) - G * (fb - fa),
        0.8 * row(s, a) + 0.1 * row(sp, a) - G * (row(dn, b) * n1),
        row(dn, a) * row(np_, a),
        G * row(dn, a),
        row(dt, a) * row(t, a),
        row(dt, a) * row(tp, a),
        G * row(dt, a),
        fa,
    ]
    return low, high


def exchange(sides, faces, links, ph, *refs):
    fields, refs = refs[:8], refs[8:]
    (
        rims_ref, ends_ref, table_ref, diag_ref, coef_ref,
        held, pack, ends, ring, ring_ends, chosen, coef,
        load_sem, coef_sem, near_send, near_recv, diag_send, diag_recv, ring_send, ring_recv, ring_ends_send, ring_ends_recv,
        main_send, main_recv, ext_send, ext_recv, corner_send, corner_recv,
    ) = refs
    last = sides - 1
    pairs = faces // 2
    side = held.shape[1]
    w = lax.axis_index("wide")
    c = lax.axis_index("narrow")
    f = w // sides
    r = w % sides
    x, half = f // 2, f % 2
    at = lambda face, row, col: (face * sides + row, col)
    signal = lambda bar, d: pl.semaphore_signal(bar, inc=1, device_id=d, device_id_type=MESH)
    is_end = lambda q: (q == 0) | (q == last)
    corner = is_end(r) & is_end(c)
    rim = is_end(r) | is_end(c)
    inside = lambda row, col: (row >= 0) & (row <= last) & (col >= 0) & (col <= last)
    edges = [(W, c == 0, r, last), (S, r == 0, c, last), (E, c == last, r, 0), (N, r == last, c, 0)]
    ext_to = lambda q: (q + 1, q - 1, last - 1 - q, last + 1 - q)
    ext_from = lambda q: (q - 1, q + 1, last - 1 - q, last + 1 - q)
    corner_at = lambda i: at(x * 2 + i // 4, (i // 2) % 2 * last, i % 2 * last)
    me_corner = half * 4 + (r // last) * 2 + c // last
    ring_at = lambda k: at((f + 2 * k) % faces, r, c)

    bar = pltpu.get_barrier_semaphore()
    awaited = jnp.int32(0)
    for e, has, q, line in edges:

        @pl.when(has)
        def _(q=q, line=line):
            for h in range(2):
                g = x * 2 + h
                for p in (q, last - q):
                    for row, col in ((p, line), (line, p)):

                        @pl.when(~((g == f) & (row == r) & (col == c)))
                        def _(g=g, row=row, col=col):
                            signal(bar, at(g, row, col))

                for p in ext_from(q):

                    @pl.when((p >= 0) & (p <= last))
                    def _(g=g, p=p):
                        signal(bar, at(g, p, line))
                        signal(bar, at(g, line, p))

        ext = jnp.where(is_end(q), 8, 16)
        awaited += jnp.where(has, 8 + ext, 0)
    own = corner & (r != c)
    awaited -= jnp.where(own, 2, 0)

    @pl.when(rim)
    def _():
        for k in range(1, pairs):
            signal(bar, ring_at(k))

    @pl.when(corner)
    def _():
        for i in range(8):

            @pl.when(i != me_corner)
            def _(i=i):
                signal(bar, corner_at(i))

    awaited += jnp.where(rim, pairs - 1, 0) + jnp.where(corner, 7, 0)
    for dr in (-1, 0, 1):
        for dc in (-1, 0, 1):
            if (dr, dc) != (0, 0):
                there = inside(r + dr, c + dc)
                awaited += there.astype(jnp.int32)

                @pl.when(there)
                def _(dr=dr, dc=dc):
                    signal(bar, at(f, r + dr, c + dc))

    loads = [pltpu.make_async_copy(ref, held.at[k], load_sem.at[k]) for k, ref in enumerate(fields)]
    for copy in loads:
        copy.start()

    which = lax.broadcasted_iota(jnp.int32, (CONSTITUENTS, side), 0)
    count = (lax.broadcasted_iota(jnp.int32, (CONSTITUENTS, side), 1) + 1).astype(jnp.float32)
    start = jnp.zeros((CONSTITUENTS, side), jnp.float32)
    rate = jnp.zeros((CONSTITUENTS, side), jnp.float32)
    for k in range(CONSTITUENTS):
        start = jnp.where(which == k, ph[k], start)
        rate = jnp.where(which == k, jnp.float32(tide_omega[k]) * jnp.float32(step_seconds), rate)
    angle = start + rate * count
    coef[0:CONSTITUENTS, :] = jnp.cos(angle)
    coef[CONSTITUENTS:, :] = jnp.sin(angle)
    keep = pltpu.make_async_copy(coef, coef_ref, coef_sem.at[0])
    keep.start()

    for copy in loads:
        copy.wait()
    sp, s, up, u, vp, v, dw, ds = (held.at[k] for k in range(8))
    lo, hi = rims(s[...], sp[...], v[...], vp[...], u[...], up[...], ds[...], dw[...])
    for k in range(LINES):
        pack[S, k : k + 1, :] = lo[k]
        pack[N, k : k + 1, :] = hi[k]
    flip = lambda ref: jnp.transpose(ref[...])
    lo, hi = rims(flip(s), flip(sp), flip(u), flip(up), flip(v), flip(vp), flip(dw), flip(ds))
    for k in range(LINES):
        pack[W, k : k + 1, :] = lo[k]
        pack[E, k : k + 1, :] = hi[k]
    for e in range(4):
        pack[e, LINES:16, :] = jnp.zeros((16 - LINES, side), jnp.float32)
    stacked = jnp.concatenate([pack[e] for e in range(4)] + [jnp.zeros((side - 64, side), jnp.float32)], axis=0)
    turned = jnp.transpose(stacked)
    lane = lax.broadcasted_iota(jnp.int32, (1, side), 1)
    for e in range(4):
        gathered = jnp.zeros((1, side), jnp.float32)
        for k, i in enumerate((0, 1, side - 2, side - 1)):
            moved = turned[i : i + 1, :]
            by = (16 * k - 16 * e) % side
            if by:
                moved = pltpu.roll(moved, by, 1)
            gathered = jnp.where((lane >= 16 * k) & (lane < 16 * k + 16), moved, gathered)
        ends[e] = gathered
        pack[e, LINES : LINES + 1, :] = gathered

    pl.semaphore_wait(bar, awaited)

    full = pl.ds(0, LINES + 1)
    block = pl.ds(0, LINES)
    here = (w, c)
    remote = lambda a, b, ss, rs, d: pltpu.make_async_remote_copy(
        a, b, ss, rs, device_id=d, device_id_type=MESH
    )
    ring_copies = lambda e: [
        remote(pack.at[e, full], ring.at[e, k, full], ring_send.at[e, k], ring_recv.at[e, k], ring_at(k))
        for k in range(1, pairs)
    ]
    ends_copies = lambda: [
        remote(ends, ring_ends.at[k], ring_ends_send.at[k], ring_ends_recv.at[k], ring_at(k)) for k in range(1, pairs)
    ]
    for e, has, q, line in edges:

        @pl.when(has)
        def _(e=e):
            for copy in ring_copies(e):
                copy.start()

    @pl.when(corner)
    def _():
        for copy in ends_copies():
            copy.start()

    near = [(E, W, 0, 1), (N, S, 1, 0), (W, E, 0, -1), (S, N, -1, 0)]
    diagonal = [(0, 1, 1), (1, 1, -1), (2, -1, 1), (3, -1, -1)]
    near_copy = lambda e, to, dr, dc: remote(
        pack.at[e, block], rims_ref.at[to, 8, block], near_send.at[e], near_recv.at[e], at(f, r + dr, c + dc)
    )
    diag_copy = lambda k, dr, dc: remote(ends, diag_ref.at[k], diag_send.at[k], diag_recv.at[k], at(f, r + dr, c + dc))
    for e, to, dr, dc in near:

        @pl.when(inside(r + dr, c + dc))
        def _(e=e, to=to, dr=dr, dc=dc):
            near_copy(e, to, dr, dc).start()

    for k, dr, dc in diagonal:

        @pl.when(inside(r + dr, c + dc))
        def _(k=k, dr=dr, dc=dc):
            diag_copy(k, dr, dc).start()

    for e, has, q, line in edges:

        @pl.when(has)
        def _(e=e):
            for copy in ring_copies(e):
                copy.wait_recv()

    for e, has, q, line in edges:
        to_ws = e in (E, N)
        kind = 1 if e in (N, S) else 0
        lines = [(h, to) for h in range(2) for to in ((W, S) if to_ws else (E, N))]

        @pl.when(has)
        def _(e=e, q=q, line=line, kind=kind, lines=lines):
            ring[e, 0] = pack[e]
            for j, (h, to) in enumerate(lines):
                far_x = links[0, to, x * 2 + h] // 2
                chosen[e, j] = ring[e, lax.rem(x - far_x + pairs, pairs)]
            for j, (h, to) in enumerate(lines):
                g = x * 2 + h
                place = lambda p, to=to: (p, line) if to in (W, E) else (line, p)
                for par, p in enumerate((q, last - q)):
                    slot = (half * 2 + kind) * 2 + par
                    row, col = place(p)
                    mine = (g == f) & (row == r) & (col == c)

                    @pl.when(~mine)
                    def _(j=j, to=to, slot=slot, g=g, row=row, col=col):
                        remote(
                            chosen.at[e, j, block], rims_ref.at[to, slot, block], main_send.at[e], main_recv.at[to], at(g, row, col)
                        ).start()

                    @pl.when(mine)
                    def _(j=j, to=to, slot=slot):
                        pltpu.make_async_copy(chosen.at[e, j, block], rims_ref.at[to, slot, block], main_recv.at[to]).start()

            for j, (h, to) in enumerate(lines):
                g = x * 2 + h
                place = lambda p, to=to: (p, line) if to in (W, E) else (line, p)
                for kind_x, p in enumerate(ext_to(q)):
                    slot = (half * 2 + kind) * 4 + kind_x
                    row, col = place(p)

                    @pl.when((p >= 0) & (p <= last))
                    def _(j=j, to=to, slot=slot, g=g, row=row, col=col):
                        remote(
                            chosen.at[e, j, pl.ds(LINES, 1)], ends_ref.at[to, slot], ext_send.at[e], ext_recv.at[to], at(g, row, col)
                        ).start()

    corner_copy = lambda i: remote(ring_ends, table_ref.at[me_corner], corner_send.at[0], corner_recv.at[0], corner_at(i))

    @pl.when(corner)
    def _():
        for copy in ends_copies():
            copy.wait_recv()
        ring_ends[0] = ends[...]
        for i in range(8):

            @pl.when(i != me_corner)
            def _(i=i):
                corner_copy(i).start()

        pltpu.make_async_copy(ring_ends, table_ref.at[me_corner], corner_recv.at[0]).start()

    take = lambda ref, ss, rs: remote(ref, ref, ss, rs, here)
    for e, to, dr, dc in near:

        @pl.when(inside(r - dr, c - dc))
        def _(e=e, to=to):
            take(rims_ref.at[to, 8, block], near_send.at[e], near_recv.at[e]).wait_recv()

    for k, dr, dc in diagonal:

        @pl.when(inside(r - dr, c - dc))
        def _(k=k):
            take(diag_ref.at[k], diag_send.at[k], diag_recv.at[k]).wait_recv()

    for e, has, q, line in edges:

        @pl.when(has)
        def _(e=e, q=q):
            take(rims_ref.at[e, pl.ds(0, 8), block], main_send.at[0], main_recv.at[e]).wait_recv()

            @pl.when(is_end(q))
            def _():
                take(ends_ref.at[e, pl.ds(0, 8)], ext_send.at[0], ext_recv.at[e]).wait_recv()

            @pl.when(~is_end(q))
            def _():
                take(ends_ref.at[e], ext_send.at[0], ext_recv.at[e]).wait_recv()

    @pl.when(corner)
    def _():
        take(table_ref, corner_send.at[0], corner_recv.at[0]).wait_recv()

    keep.wait()
    for e, to, dr, dc in near:

        @pl.when(inside(r + dr, c + dc))
        def _(e=e, to=to, dr=dr, dc=dc):
            near_copy(e, to, dr, dc).wait_send()

    for k, dr, dc in diagonal:

        @pl.when(inside(r + dr, c + dc))
        def _(k=k, dr=dr, dc=dc):
            diag_copy(k, dr, dc).wait_send()

    for e, has, q, line in edges:

        @pl.when(has)
        def _(e=e, q=q):
            for copy in ring_copies(e):
                copy.wait_send()

            @pl.when(~own)
            def _():
                take(rims_ref.at[e, pl.ds(0, 8), block], main_send.at[e], main_recv.at[e]).wait_send()

            @pl.when(own)
            def _():
                take(rims_ref.at[e, pl.ds(0, 7), block], main_send.at[e], main_recv.at[e]).wait_send()

            @pl.when(is_end(q))
            def _():
                take(ends_ref.at[e, pl.ds(0, 8)], ext_send.at[e], ext_recv.at[e]).wait_send()

            @pl.when(~is_end(q))
            def _():
                take(ends_ref.at[e], ext_send.at[e], ext_recv.at[e]).wait_send()

    @pl.when(corner)
    def _():
        for copy in ends_copies():
            copy.wait_send()
        take(table_ref.at[pl.ds(0, 7)], corner_send.at[0], corner_recv.at[0]).wait_send()


def substeps(
    sides, faces, links, *refs
):
    fields, refs = refs[:8], refs[8:]
    (
        rims_ref, ends_ref, cx_ref, dx_ref, coef_ref, s_out, u_out, v_out, h_out,
        held, mains, exts, cx, dx, coef, levels, sums, load_sem, main_sem, ext_sem, table_sem, out_sem, sum_sem,
    ) = refs
    last = sides - 1
    side = held.shape[1]
    link = lambda face, edge, k: links[k, edge, face]
    w = lax.axis_index("wide")
    c = lax.axis_index("narrow")
    f = w // sides
    r = w % sides
    lane = lax.broadcasted_iota(jnp.int32, (1, side), 1)
    rows = lax.broadcasted_iota(jnp.int32, (side, side), 0)
    cols = lax.broadcasted_iota(jnp.int32, (side, side), 1)
    mirror = (rows + cols == side - 1).astype(jnp.float32)
    diagonal = rows == cols
    pick = lambda cond, a, b: jnp.where(cond, a, b)
    up_by = lambda x, fill: jnp.where(lane == side - 1, fill, pltpu.roll(x, side - 1, 1))
    down_by = lambda x, fill: jnp.where(lane == 0, fill, pltpu.roll(x, 1, 1))
    head = lambda x: x[:, 0:1]
    tail = lambda x: x[:, side - 1 : side]

    def end(x, k, line):
        return x[:, 16 * k + line : 16 * k + line + 1]

    def corner_of(face, edge, high):
        row = jnp.where(edge == S, 0, jnp.where(edge == N, 1, high))
        col = jnp.where(edge == W, 0, jnp.where(edge == E, 1, high))
        pairs = faces // 2
        return cx[face % 2 * 4 + row * 2 + col, lax.rem(f // 2 - face // 2 + pairs, pairs), edge]

    def at_end(x, high, k, line):
        return pick(high == 1, end(x, 3 - k, line), end(x, k, line))

    def beyond(face, edge, high):
        far, far_edge, turn = (link(face, edge, k) for k in range(3))
        stop = high ^ turn
        return at_end(corner_of(far, far_edge, stop), stop, 0, 8)

    def at_corner(face, edge, low_end, inner):
        vertical = (edge == W) | (edge == E)
        side_edge = jnp.where(vertical, S, W) if low_end else jnp.where(vertical, N, E)
        start = (edge >= E).astype(jnp.int32)
        far, far_edge, turn = (link(face, side_edge, k) for k in range(3))
        high = start ^ turn
        x = corner_of(far, far_edge, high)
        far_vertical = (far_edge == W) | (far_edge == E)
        third = beyond(far, jnp.where(far_vertical, N, E), (far_edge >= E).astype(jnp.int32))
        ahead = pick(high == 1, third, end(x, 1, 5))
        s1 = at_end(x, high, 0, 1) - G * (ahead - at_end(x, high, 0, 5))
        got = dict(s0=at_end(x, high, 0, 0), s1=s1)
        if low_end:
            got["s1"] = s1 - G * inner
        else:
            got.update(
                T0=at_end(x, high, 0, 8),
                Q=at_end(x, high, 0, 3),
                D=at_end(x, high, 0, 4),
                Tb=at_end(x, high, 1, 8),
            )
        return got

    def place(edge, to_ws):
        on_face = {W: c == 0, S: r == 0, E: c == last, N: r == last}[edge]
        across = edge in (W, E)
        seg = r if across else c
        face, partner, turn = (link(f, edge, k) for k in range(3))
        flipped = on_face & (turn == 1)
        kind = (partner == (N if to_ws else S)).astype(jnp.int32)
        q = jnp.where(turn == 1, last - seg, seg)
        slot = jnp.where(on_face, (face % 2 * 2 + kind) * 2 + turn, 8)
        slot_x = jnp.where(on_face, (face % 2 * 2 + kind) * 4 + 2 * turn, 0)
        return on_face, face, partner, flipped, q, slot, slot_x

    places = {e: place(e, e in (W, S)) for e in range(4)}
    loads = [pltpu.make_async_copy(x, held.at[k], load_sem.at[k]) for k, x in enumerate(fields)]
    tables = [
        pltpu.make_async_copy(a, b, table_sem.at[k])
        for k, (a, b) in enumerate(((cx_ref, cx), (dx_ref, dx), (coef_ref, coef)))
    ]
    arrivals = []
    for e in range(4):
        slot, slot_x = places[e][5:]
        arrivals.append(pltpu.make_async_copy(rims_ref.at[e, slot], mains.at[e], main_sem.at[e]))
        for k in range(2):
            arrivals.append(pltpu.make_async_copy(ends_ref.at[e, slot_x + k], exts.at[e, k], ext_sem.at[e, k]))
    for copy in arrivals + tables + loads:
        copy.start()
    for copy in arrivals + tables:
        copy.wait()

    def ghost(edge, to_ws):
        on_face, face, partner, flipped, q, slot, slot_x = places[edge]
        block = mains[edge]
        line = [block[k : k + 1, :] for k in range(LINES)]
        strip = (edge + 2) % 4
        lo_at, hi_at = {W: (0, 2), S: (0, 1), E: (1, 3), N: (2, 3)}[edge]
        lo_x = pick(on_face, exts[edge, 0], dx[lo_at, strip])
        hi_x = pick(on_face, exts[edge, 1], dx[hi_at, strip])
        first = head(line[5])
        lo = dict(
            s0=end(lo_x, 3, 0), s1=end(lo_x, 3, 1) - G * (first - end(lo_x, 3, 5)),
            F=end(lo_x, 3, 8), R=end(lo_x, 3, 3), Dn=end(lo_x, 3, 4), Fb=end(lo_x, 2, 8),
        )
        hi = dict(
            s0=end(hi_x, 0, 0), s1=end(hi_x, 0, 1) - G * (end(hi_x, 1, 5) - end(hi_x, 0, 5)),
            T0=end(hi_x, 0, 5), Q=end(hi_x, 0, 6), D=end(hi_x, 0, 7), Tb=end(hi_x, 0, 8),
            F=end(hi_x, 0, 8), R=end(hi_x, 0, 3), Dn=end(hi_x, 0, 4), Fb=end(hi_x, 1, 8),
        )
        lo_corner = on_face & (q == 0)
        hi_corner = on_face & (q == last)
        safe = lambda x, top: jnp.where(on_face, x, top)
        g_face, g_edge = safe(face, 0), safe(partner, E if to_ws else W)
        third_lo = at_corner(g_face, g_edge, True, first)
        third_hi = at_corner(g_face, g_edge, False, first)
        for name, value in third_lo.items():
            lo[name] = pick(lo_corner, value, lo[name])
        for name, value in third_hi.items():
            hi[name] = pick(hi_corner, value, hi[name])
        lo["done"], hi["done"] = lo_corner, hi_corner
        turned = jnp.dot(block, mirror, precision=lax.Precision.HIGHEST, preferred_element_type=jnp.float32)
        turned = [turned[k : k + 1, :] for k in range(LINES)]
        along = {5: ("T0", -1.0), 6: ("Q", -1.0), 7: ("D", 1.0)}
        if to_ws:
            along[8] = ("Tb", -1.0)
        out = []
        for k in range(LINES):
            if k in along:
                name, sign = along[k]
                other = sign * down_by(turned[k], hi[name])
            else:
                other = turned[k]
            out.append(pick(flipped, other, line[k]))
        new_lo = {n: pick(flipped, hi[n], lo[n]) for n in ("s0", "s1", "F", "R", "Dn", "Fb")}
        new_hi = {n: pick(flipped, lo[n], hi[n]) for n in ("s0", "s1", "F", "R", "Dn", "Fb")}
        for k, (name, sign) in along.items():
            new_hi[name] = pick(flipped, sign * head(line[k]), hi[name])
        new_lo["done"] = jnp.where(flipped, hi_corner, lo_corner)
        new_hi["done"] = jnp.where(flipped, lo_corner, hi_corner)
        return out, new_lo, new_hi

    (wl, w_lo, w_hi), (sl, s_lo, s_hi) = ghost(W, True), ghost(S, True)
    (el, e_lo, e_hi), (nl, n_lo, n_hi) = ghost(E, False), ghost(N, False)

    for d, x in ((w_lo, sl), (w_hi, nl), (s_lo, wl), (s_hi, el)):
        d["s1"] = pick(d["done"], d["s1"], d["s1"] - G * head(x[5]))

    west, south, east, north = c == 0, r == 0, c == last, r == last
    take_w, take_s = west & ~south, south & ~west
    sw_w = {n: pick(take_s, s_lo[n], w_lo[n]) for n in ("s0", "s1")}
    sw_s = {n: pick(take_w, w_lo[n], s_lo[n]) for n in ("s0", "s1")}
    w_lo.update(sw_w)
    s_lo.update(sw_s)
    share = (("s0", "s0"), ("s1", "s1"), ("T0", "F"), ("Q", "R"), ("D", "Dn"), ("Tb", "Fb"))
    take_e, take_s = east & ~south, south & ~east
    se_s = {a: pick(take_e, e_lo[b], s_hi[a]) for a, b in share}
    e_lo["s0"] = pick(take_s, s_hi["s0"], e_lo["s0"])
    s_hi.update(se_s)
    take_n, take_w = north & ~west, west & ~north
    nw_w = {a: pick(take_n, n_lo[b], w_hi[a]) for a, b in share}
    n_lo["s0"] = pick(take_w, w_hi["s0"], n_lo["s0"])
    w_hi.update(nw_w)
    take_e, take_n = east & ~north, north & ~east
    share = (("s0", "s0"), ("T0", "F"), ("Q", "R"), ("D", "Dn"))
    ne_n = {a: pick(take_e, e_hi[b], n_hi[a]) for a, b in share}
    ne_e = {a: pick(take_n, n_hi[b], e_hi[a]) for a, b in share}
    n_hi.update(ne_n)
    e_hi.update(ne_e)

    class HeightRim:
        def __init__(self, line, lo, hi):
            self.line, self.lo, self.hi = line, lo, hi

        def at(self, n, flux):
            s0, y1, y2, z, back, t0, q, d, tb = self.line
            lo, hi = self.lo, self.hi
            if n == 0:
                return s0
            if n == 1:
                self.s1 = y1 - G * flux - G * (up_by(t0, hi["T0"]) - t0)
                return self.s1
            if n == 2:
                self.t1 = q - d * (s0 - down_by(s0, lo["s0"]))
                self.t1hi = hi["Q"] - hi["D"] * (hi["s0"] - tail(s0))
                self.s2 = y2 + 0.1 * self.s1 - G * flux - G * (up_by(self.t1, self.t1hi) - self.t1)
                return self.s2
            s1 = self.s1
            t2 = 0.8 * t0 + 0.1 * q + 0.1 * self.t1 - d * (s1 - down_by(s1, lo["s1"]))
            t2hi = 0.8 * hi["T0"] + 0.1 * hi["Q"] + 0.1 * self.t1hi - hi["D"] * (hi["s1"] - tail(s1))
            inner = s1 + G * (up_by(tb, hi["Tb"]) - tb)
            return 0.81 * s1 + 0.1 * self.s2 + z - G * back * inner - G * flux - G * (up_by(t2, t2hi) - t2)

    class FluxRim:
        def __init__(self, line, lo, hi):
            self.line, self.lo, self.hi = line, lo, hi

        def at(self, n, height):
            s0, u1, u2, r_, d_, t0, q, d, f0 = self.line
            lo, hi = self.lo, self.hi
            if n == 0:
                return f0
            if n == 1:
                self.f1 = r_ - d_ * (s0 - height)
                return self.f1
            if n == 2:
                self.s1 = u1 - G * (up_by(t0, hi["T0"]) - t0)
                self.older = 0.8 * f0 + 0.1 * r_ + 0.1 * self.f1
                self.f2 = self.older - d_ * (self.s1 - height)
                return self.f2
            t1 = q - d * (s0 - down_by(s0, lo["s0"]))
            t1hi = hi["Q"] - hi["D"] * (hi["s0"] - tail(s0))
            s2 = u2 + 0.1 * self.s1 + G * self.f1 - G * (up_by(t1, t1hi) - t1)
            return 0.8 * self.f1 + 0.1 * self.f2 + 0.1 * self.older - d_ * (s2 - height)

    rim_w, rim_s = HeightRim(wl, w_lo, w_hi), HeightRim(sl, s_lo, s_hi)
    rim_e, rim_n = FluxRim(el, e_lo, e_hi), FluxRim(nl, n_lo, n_hi)
    as_row = lambda col: jnp.sum(jnp.where(diagonal, col, 0.0), axis=0, keepdims=True)
    as_col = lambda row: jnp.sum(jnp.where(diagonal, row, 0.0), axis=1, keepdims=True)
    for copy in loads:
        copy.wait()
    sp_, s_, up_, u_, vp_, v_, dw_, ds_ = (held[k] for k in range(8))
    first_col, last_col = cols == 0, cols == side - 1
    first_row, last_row = rows == 0, rows == side - 1
    flux_w = flux_s = height_e = height_n = None
    snaps = []
    for n in range(SUBSTEPS):
        fw, fs = dw_ * u_, ds_ * v_
        west_line, south_line = rim_w.at(n, flux_w), rim_s.at(n, flux_s)
        east_line, north_line = rim_e.at(n, height_e), rim_n.at(n, height_n)
        flux_w, flux_s = as_row(fw[:, 0:1]), fs[0:1, :]
        height_e, height_n = as_row(s_[:, side - 1 : side]), s_[side - 1 : side, :]
        fe = jnp.where(last_col, as_col(east_line), pltpu.roll(fw, side - 1, 1))
        fn = jnp.where(last_row, north_line, pltpu.roll(fs, side - 1, 0))
        sw = jnp.where(first_col, as_col(west_line), pltpu.roll(s_, 1, 1))
        ss = jnp.where(first_row, south_line, pltpu.roll(s_, 1, 0))
        s_next = sp_ - G * ((fe - fw) + (fn - fs))
        u_next = up_ - G * (s_ - sw)
        v_next = vp_ - G * (s_ - ss)
        sp_ = s_ + 0.1 * (sp_ - 2.0 * s_ + s_next)
        up_ = u_ + 0.1 * (up_ - 2.0 * u_ + u_next)
        vp_ = v_ + 0.1 * (vp_ - 2.0 * v_ + v_next)
        s_, u_, v_ = s_next, u_next, v_next
        snaps.append(s_)
    stores = []
    for k, (x, out) in enumerate(((s_, s_out), (u_, u_out), (v_, v_out))):
        levels[k] = x
        stores.append(pltpu.make_async_copy(levels.at[k], out, out_sem.at[k]))
        stores[-1].start()
    for k in range(2 * CONSTITUENTS):
        total = coef[k : k + 1, 0:1] * snaps[0]
        for n in range(1, SUBSTEPS):
            total += coef[k : k + 1, n : n + 1] * snaps[n]
        sums[k] = total
        stores.append(pltpu.make_async_copy(sums.at[k], h_out.at[k], sum_sem.at[k]))
        stores[-1].start()
    for copy in stores:
        copy.wait()


def solution(mesh):
    def body(sp, s, up, u, vp, v, dw, ds, links, ph):
        side = s.shape[0]
        sides = mesh.shape["narrow"]
        faces = mesh.shape["wide"] // sides
        f32 = jnp.float32
        shape = lambda *dims: jax.ShapeDtypeStruct(dims, f32)
        hbm = pl.BlockSpec(memory_space=pl.ANY)
        smem = pl.BlockSpec(memory_space=pltpu.SMEM)
        dma = pltpu.SemaphoreType.DMA
        links = jnp.transpose(links, (2, 1, 0))
        got = pl.pallas_call(
            functools.partial(exchange, sides, faces),
            out_shape=(
                shape(4, 9, 16, side),
                shape(4, 16, 1, side),
                shape(8, faces // 2, 4, 1, side),
                shape(4, 4, 1, side),
                shape(2 * CONSTITUENTS, side),
            ),
            in_specs=[smem] * 2 + [hbm] * 8,
            out_specs=(hbm,) * 5,
            scratch_shapes=[
                pltpu.VMEM((8, side, side), f32),
                pltpu.VMEM((4, 16, side), f32),
                pltpu.VMEM((4, 1, side), f32),
                pltpu.VMEM((4, faces // 2, 16, side), f32),
                pltpu.VMEM((faces // 2, 4, 1, side), f32),
                pltpu.VMEM((4, 4, 16, side), f32),
                pltpu.VMEM((2 * CONSTITUENTS, side), f32),
                dma((8,)), dma((1,)), dma((4,)), dma((4,)), dma((4,)), dma((4,)),
                dma((4, faces // 2)), dma((4, faces // 2)), dma((faces // 2,)), dma((faces // 2,)),
                dma((4,)), dma((4,)), dma((4,)), dma((4,)), dma((1,)), dma((1,)),
            ],
            compiler_params=pltpu.CompilerParams(collective_id=0, has_side_effects=True),
        )(links, ph, sp, s, up, u, vp, v, dw, ds)
        tile = shape(side, side)
        return pl.pallas_call(
            functools.partial(substeps, sides, faces),
            out_shape=(tile, tile, tile, shape(2 * CONSTITUENTS, side, side)),
            in_specs=[smem] + [hbm] * 13,
            out_specs=(hbm,) * 4,
            scratch_shapes=[
                pltpu.VMEM((8, side, side), f32),
                pltpu.VMEM((4, 16, side), f32),
                pltpu.VMEM((4, 2, 1, side), f32),
                pltpu.VMEM((8, faces // 2, 4, 1, side), f32),
                pltpu.VMEM((4, 4, 1, side), f32),
                pltpu.VMEM((2 * CONSTITUENTS, side), f32),
                pltpu.VMEM((3, side, side), f32),
                pltpu.VMEM((2 * CONSTITUENTS, side, side), f32),
                dma((8,)),
                dma((4,)),
                dma((4, 2)),
                dma((3,)),
                dma((3,)),
                dma((2 * CONSTITUENTS,)),
            ],
        )(links, sp, s, up, u, vp, v, dw, ds, *got)

    tiles = P("wide", "narrow")
    return jax.shard_map(
        body,
        mesh=mesh,
        in_specs=(tiles,) * 8 + (P(), P()),
        out_specs=(tiles, tiles, tiles, P(None, "wide", "narrow")),
        check_vma=False,
    )
```

time: 47.1 us -> 36.8 us (0.78)
  Pallas kernels: 44.8 us -> 35.9 us
  local copies, waits for them, and re-layouts: 1.39 us -> 0 us
    pallas_call x1, Pallas kernels: 40.2 us -> 30.3 us  [body(): pl.pallas_call(functools.partial(exchange, sides, faces), out_shape=(shap...]
    unnamed x1 -> x0, local copies, waits for them, and re-layouts: 1.39 us -> none
    pallas_call x1, Pallas kernels: 4.59 us -> 5.56 us  [body(): pl.pallas_call(functools.partial(substeps, sides, faces), out_shape=(tile...]
where the time goes in v2:
time: 36.8 us; the launch traced here: 36.5 us
  Pallas kernels  35.9 us (98%)
  between operations  0.64 us (2%)
    pallas_call x1, Pallas kernels, body(): pl.pallas_call(functools.partial(exchange, sides, faces), out_shape=(shap...  30.3 us
    pallas_call x1, Pallas kernels, body(): pl.pallas_call(functools.partial(substeps, sides, faces), out_shape=(tile...  5.56 us

profile of v2, /device:TPU:1, one launch (start us, length us, event | category | flops | bytes accessed | tf_op | source)
XLA Modules:
  0.0 36.5 jit_solution(2023158344521436972)
XLA Ops:
  0.6 30.3 %shard_map.129 = (f32[4,9,16,128]{3,2,1,0:T(8,128)}, f32[4,16,1,128]{3,2,1,0:T(1,128)}, f32[8,4,4,1,128]{4,3,2,1,0:T(1,128)}, f32[4,4,1,128]{3,2,1,0:T(1,128)}, f32[16,128]{1,0:T(8,128)}) custom-call(s32[3,4,8]{2,1,0:T(4,128)} %bitcast.1, f32[8]{0:T(128)} %ph.1, f32[128,128]{1,0:T(8,128)} %refs_0_.3, f32[128,128]{1,0:T(8,128)} %refs_1_.3, ...), custom_call_target="tpu_custom_call" | custom-call | tf_op jit(solution)/shard_map/pallas_call | solution.py:651
  30.9 5.6 %shard_map.130 = (f32[128,128]{1,0:T(8,128)}, f32[128,128]{1,0:T(8,128)}, f32[128,128]{1,0:T(8,128)}, f32[16,128,128]{2,1,0:T(8,128)}) custom-call(s32[3,4,8]{2,1,0:T(4,128)} %bitcast.2, f32[128,128]{1,0:T(8,128)} %refs_0_.3, f32[128,128]{1,0:T(8,128)} %refs_1_.3, f32[128,128]{1,0:T(8,128)} %refs_2_.3, f32[128,128]{1,0:T(8,128)} %refs_3_.3, ...), custom_call_target="tpu_custom_call" | custom-call | tf_op jit(solution)/shard_map/pallas_call | solution.py:677

commit v3 on v2

--- a/solution.py
+++ b/solution.py
@@ -66,12 +66,13 @@
     return low, high
 
 
-def exchange(sides, faces, links, ph, *refs):
+def exchange(sides, faces, links_ref, ph_ref, *refs):
     fields, refs = refs[:8], refs[8:]
     (
-        rims_ref, ends_ref, table_ref, diag_ref, coef_ref,
-        held, pack, ends, ring, ring_ends, chosen, coef,
-        load_sem, coef_sem, near_send, near_recv, diag_send, diag_recv, ring_send, ring_recv, ring_ends_send, ring_ends_recv,
+        picked, coef,
+        links, ph, rims_ref, ends_ref, table_ref, diag_ref,
+        held, pack, ends, ring, ring_ends, chosen,
+        load_sem, links_sem, near_send, near_recv, diag_send, diag_recv, ring_send, ring_recv, ring_ends_send, ring_ends_recv,
         main_send, main_recv, ext_send, ext_recv, corner_send, corner_recv,
     ) = refs
     last = sides - 1
@@ -146,9 +147,14 @@
                 def _(dr=dr, dc=dc):
                     signal(bar, at(f, r + dr, c + dc))
 
-    loads = [pltpu.make_async_copy(ref, held.at[k], load_sem.at[k]) for k, ref in enumerate(fields)]
+    loads = [
+        pltpu.make_async_copy(ph_ref, ph, links_sem.at[0]),
+        pltpu.make_async_copy(links_ref, links, links_sem.at[1]),
+    ] + [pltpu.make_async_copy(ref, held.at[k], load_sem.at[k]) for k, ref in enumerate(fields)]
     for copy in loads:
         copy.start()
+    for copy in loads:
+        copy.wait()
 
     which = lax.broadcasted_iota(jnp.int32, (CONSTITUENTS, side), 0)
     count = (lax.broadcasted_iota(jnp.int32, (CONSTITUENTS, side), 1) + 1).astype(jnp.float32)
@@ -160,24 +166,21 @@
     angle = start + rate * count
     coef[0:CONSTITUENTS, :] = jnp.cos(angle)
     coef[CONSTITUENTS:, :] = jnp.sin(angle)
-    keep = pltpu.make_async_copy(coef, coef_ref, coef_sem.at[0])
-    keep.start()
-
-    for copy in loads:
-        copy.wait()
+
     sp, s, up, u, vp, v, dw, ds = (held.at[k] for k in range(8))
     lo, hi = rims(s[...], sp[...], v[...], vp[...], u[...], up[...], ds[...], dw[...])
     for k in range(LINES):
-        pack[S, k : k + 1, :] = lo[k]
-        pack[N, k : k + 1, :] = hi[k]
+        pack[S, 0, k : k + 1, :] = lo[k]
+        pack[N, 0, k : k + 1, :] = hi[k]
     flip = lambda ref: jnp.transpose(ref[...])
     lo, hi = rims(flip(s), flip(sp), flip(u), flip(up), flip(v), flip(vp), flip(dw), flip(ds))
     for k in range(LINES):
-        pack[W, k : k + 1, :] = lo[k]
-        pack[E, k : k + 1, :] = hi[k]
+        pack[W, 0, k : k + 1, :] = lo[k]
+        pack[E, 0, k : k + 1, :] = hi[k]
     for e in range(4):
-        pack[e, LINES:16, :] = jnp.zeros((16 - LINES, side), jnp.float32)
-    stacked = jnp.concatenate([pack[e] for e in range(4)] + [jnp.zeros((side - 64, side), jnp.float32)], axis=0)
+        pack[e, 0, LINES:16, :] = jnp.full((16 - LINES, side), G, jnp.float32)
+    whole = jnp.concatenate([pack[e, 0] for e in range(4)], axis=0)
+    stacked = jnp.concatenate([whole, jnp.zeros((side - 64, side), jnp.float32)], axis=0)
     turned = jnp.transpose(stacked)
     lane = lax.broadcasted_iota(jnp.int32, (1, side), 1)
     for e in range(4):
@@ -189,18 +192,29 @@
                 moved = pltpu.roll(moved, by, 1)
             gathered = jnp.where((lane >= 16 * k) & (lane < 16 * k + 16), moved, gathered)
         ends[e] = gathered
-        pack[e, LINES : LINES + 1, :] = gathered
+        for k in range(2):
+            pack[e, k, LINES : LINES + 1, :] = gathered
+    total = lax.broadcasted_iota(jnp.int32, (side, side), 0) + lax.broadcasted_iota(jnp.int32, (side, side), 1)
+    mirror = (total == side - 1).astype(jnp.float32)
+    turned = jnp.dot(whole, mirror, precision=lax.Precision.HIGHEST, preferred_element_type=jnp.float32)
+    for e in range(4):
+        for k in range(LINES):
+            line_k = turned[16 * e + k : 16 * e + k + 1, :]
+            if k in (5, 6, 7) or (k == 8 and e in (E, N)):
+                line_k = jnp.where(lane == 0, 0.0, pltpu.roll(line_k, 1, 1))
+                line_k = line_k if k == 7 else -line_k
+            pack[e, 1, k : k + 1, :] = line_k
 
     pl.semaphore_wait(bar, awaited)
 
     full = pl.ds(0, LINES + 1)
-    block = pl.ds(0, LINES)
+    block = full
     here = (w, c)
     remote = lambda a, b, ss, rs, d: pltpu.make_async_remote_copy(
         a, b, ss, rs, device_id=d, device_id_type=MESH
     )
     ring_copies = lambda e: [
-        remote(pack.at[e, full], ring.at[e, k, full], ring_send.at[e, k], ring_recv.at[e, k], ring_at(k))
+        remote(pack.at[e, :, full], ring.at[e, k, :, full], ring_send.at[e, k], ring_recv.at[e, k], ring_at(k))
         for k in range(1, pairs)
     ]
     ends_copies = lambda: [
@@ -221,7 +235,7 @@
     near = [(E, W, 0, 1), (N, S, 1, 0), (W, E, 0, -1), (S, N, -1, 0)]
     diagonal = [(0, 1, 1), (1, 1, -1), (2, -1, 1), (3, -1, -1)]
     near_copy = lambda e, to, dr, dc: remote(
-        pack.at[e, block], rims_ref.at[to, 8, block], near_send.at[e], near_recv.at[e], at(f, r + dr, c + dc)
+        pack.at[e, 0, block], rims_ref.at[to, 8, block], near_send.at[e], near_recv.at[e], at(f, r + dr, c + dc)
     )
     diag_copy = lambda k, dr, dc: remote(ends, diag_ref.at[k], diag_send.at[k], diag_recv.at[k], at(f, r + dr, c + dc))
     for e, to, dr, dc in near:
@@ -253,7 +267,7 @@
             ring[e, 0] = pack[e]
             for j, (h, to) in enumerate(lines):
                 far_x = links[0, to, x * 2 + h] // 2
-                chosen[e, j] = ring[e, lax.rem(x - far_x + pairs, pairs)]
+                chosen[e, j] = ring[e, lax.rem(x - far_x + pairs, pairs), links[2, to, x * 2 + h]]
             for j, (h, to) in enumerate(lines):
                 g = x * 2 + h
                 place = lambda p, to=to: (p, line) if to in (W, E) else (line, p)
@@ -331,7 +345,64 @@
     def _():
         take(table_ref, corner_send.at[0], corner_recv.at[0]).wait_recv()
 
-    keep.wait()
+    link = lambda face, edge, k: links[k, edge, face]
+    end = lambda row, k, line: row[:, 16 * k + line : 16 * k + line + 1]
+    at_end = lambda row, high, k, line: jnp.where(high == 1, end(row, 3 - k, line), end(row, k, line))
+
+    def corner_of(face, edge, high):
+        row = jnp.where(edge == S, 0, jnp.where(edge == N, 1, high))
+        col = jnp.where(edge == W, 0, jnp.where(edge == E, 1, high))
+        return table_ref[face % 2 * 4 + row * 2 + col, lax.rem(x - face // 2 + pairs, pairs), edge]
+
+    def beyond(face, edge, high):
+        far, far_edge, turn = (link(face, edge, k) for k in range(3))
+        stop = high ^ turn
+        return at_end(corner_of(far, far_edge, stop), stop, 0, 8)
+
+    def at_corner(face, edge, low_end):
+        vertical = (edge == W) | (edge == E)
+        side_edge = jnp.where(vertical, S, W) if low_end else jnp.where(vertical, N, E)
+        start = (edge >= E).astype(jnp.int32)
+        far, far_edge, turn = (link(face, side_edge, k) for k in range(3))
+        high = start ^ turn
+        row = corner_of(far, far_edge, high)
+        far_vertical = (far_edge == W) | (far_edge == E)
+        third = beyond(far, jnp.where(far_vertical, N, E), (far_edge >= E).astype(jnp.int32))
+        ahead = jnp.where(high == 1, third, end(row, 1, 5))
+        s1 = at_end(row, high, 0, 1) - G * (ahead - at_end(row, high, 0, 5))
+        if low_end:
+            parts = {(3, 0): at_end(row, high, 0, 0), (3, 1): s1}
+        else:
+            parts = {(0, 0): at_end(row, high, 0, 0)}
+            across = at_end(row, high, 0, 8)
+            parts.update({(0, 1): s1, (0, 5): across, (1, 5): across, (0, 6): at_end(row, high, 0, 3)})
+            parts.update({(0, 7): at_end(row, high, 0, 4), (0, 8): at_end(row, high, 1, 8)})
+        made = jnp.zeros((1, side), jnp.float32)
+        for (k, line), value in parts.items():
+            made = jnp.where(lane == 16 * k + line, value, made)
+        return made
+
+    for e, on_face, seg, _ in edges:
+        to_ws = e in (W, S)
+        across = e in (W, E)
+        face, partner, turn = (link(f, e, k) for k in range(3))
+        kind = (partner == (N if to_ws else S)).astype(jnp.int32)
+        q = jnp.where(turn == 1, last - seg, seg)
+        slot = jnp.where(on_face, (face % 2 * 2 + kind) * 2 + turn, 8)
+        slot_x = jnp.where(on_face, (face % 2 * 2 + kind) * 4 + 2 * turn, 0)
+        strip = (e + 2) % 4
+        lo_at, hi_at = {W: (0, 2), S: (0, 1), E: (1, 3), N: (2, 3)}[e]
+        picked[e] = rims_ref[e, slot]
+        picked[e, 10:11, :] = jnp.where(on_face, ends_ref[e, slot_x], diag_ref[lo_at, strip])
+        picked[e, 11:12, :] = jnp.where(on_face, ends_ref[e, slot_x + 1], diag_ref[hi_at, strip])
+        flag = jnp.where(on_face, turn, 0).astype(jnp.float32)
+        picked[e, 12:13, :] = jnp.zeros((1, side), jnp.float32) + flag
+
+        @pl.when(corner & on_face)
+        def _(e=e, face=face, partner=partner, q=q):
+            picked[e, 10:11, :] = jnp.where(q == 0, at_corner(face, partner, True), picked[e, 10:11, :])
+            picked[e, 11:12, :] = jnp.where(q == last, at_corner(face, partner, False), picked[e, 11:12, :])
+
     for e, to, dr, dc in near:
 
         @pl.when(inside(r + dr, c + dc))
@@ -374,156 +445,54 @@
         take(table_ref.at[pl.ds(0, 7)], corner_send.at[0], corner_recv.at[0]).wait_send()
 
 
-def substeps(
-    sides, faces, links, *refs
-):
+def substeps(sides, picked, coef, *refs):
     fields, refs = refs[:8], refs[8:]
-    (
-        rims_ref, ends_ref, cx_ref, dx_ref, coef_ref, s_out, u_out, v_out, h_out,
-        held, mains, exts, cx, dx, coef, levels, sums, load_sem, main_sem, ext_sem, table_sem, out_sem, sum_sem,
-    ) = refs
+    s_out, u_out, v_out, h_out, levels, sums, out_sem, sum_sem = refs
     last = sides - 1
-    side = held.shape[1]
-    link = lambda face, edge, k: links[k, edge, face]
-    w = lax.axis_index("wide")
+    side = levels.shape[1]
     c = lax.axis_index("narrow")
-    f = w // sides
-    r = w % sides
+    r = lax.rem(lax.axis_index("wide"), sides)
     lane = lax.broadcasted_iota(jnp.int32, (1, side), 1)
     rows = lax.broadcasted_iota(jnp.int32, (side, side), 0)
     cols = lax.broadcasted_iota(jnp.int32, (side, side), 1)
-    mirror = (rows + cols == side - 1).astype(jnp.float32)
     diagonal = rows == cols
     pick = lambda cond, a, b: jnp.where(cond, a, b)
     up_by = lambda x, fill: jnp.where(lane == side - 1, fill, pltpu.roll(x, side - 1, 1))
     down_by = lambda x, fill: jnp.where(lane == 0, fill, pltpu.roll(x, 1, 1))
     head = lambda x: x[:, 0:1]
     tail = lambda x: x[:, side - 1 : side]
-
-    def end(x, k, line):
-        return x[:, 16 * k + line : 16 * k + line + 1]
-
-    def corner_of(face, edge, high):
-        row = jnp.where(edge == S, 0, jnp.where(edge == N, 1, high))
-        col = jnp.where(edge == W, 0, jnp.where(edge == E, 1, high))
-        pairs = faces // 2
-        return cx[face % 2 * 4 + row * 2 + col, lax.rem(f // 2 - face // 2 + pairs, pairs), edge]
-
-    def at_end(x, high, k, line):
-        return pick(high == 1, end(x, 3 - k, line), end(x, k, line))
-
-    def beyond(face, edge, high):
-        far, far_edge, turn = (link(face, edge, k) for k in range(3))
-        stop = high ^ turn
-        return at_end(corner_of(far, far_edge, stop), stop, 0, 8)
-
-    def at_corner(face, edge, low_end, inner):
-        vertical = (edge == W) | (edge == E)
-        side_edge = jnp.where(vertical, S, W) if low_end else jnp.where(vertical, N, E)
-        start = (edge >= E).astype(jnp.int32)
-        far, far_edge, turn = (link(face, side_edge, k) for k in range(3))
-        high = start ^ turn
-        x = corner_of(far, far_edge, high)
-        far_vertical = (far_edge == W) | (far_edge == E)
-        third = beyond(far, jnp.where(far_vertical, N, E), (far_edge >= E).astype(jnp.int32))
-        ahead = pick(high == 1, third, end(x, 1, 5))
-        s1 = at_end(x, high, 0, 1) - G * (ahead - at_end(x, high, 0, 5))
-        got = dict(s0=at_end(x, high, 0, 0), s1=s1)
-        if low_end:
-            got["s1"] = s1 - G * inner
-        else:
-            got.update(
-                T0=at_end(x, high, 0, 8),
-                Q=at_end(x, high, 0, 3),
-                D=at_end(x, high, 0, 4),
-                Tb=at_end(x, high, 1, 8),
-            )
-        return got
-
-    def place(edge, to_ws):
-        on_face = {W: c == 0, S: r == 0, E: c == last, N: r == last}[edge]
-        across = edge in (W, E)
-        seg = r if across else c
-        face, partner, turn = (link(f, edge, k) for k in range(3))
-        flipped = on_face & (turn == 1)
-        kind = (partner == (N if to_ws else S)).astype(jnp.int32)
-        q = jnp.where(turn == 1, last - seg, seg)
-        slot = jnp.where(on_face, (face % 2 * 2 + kind) * 2 + turn, 8)
-        slot_x = jnp.where(on_face, (face % 2 * 2 + kind) * 4 + 2 * turn, 0)
-        return on_face, face, partner, flipped, q, slot, slot_x
-
-    places = {e: place(e, e in (W, S)) for e in range(4)}
-    loads = [pltpu.make_async_copy(x, held.at[k], load_sem.at[k]) for k, x in enumerate(fields)]
-    tables = [
-        pltpu.make_async_copy(a, b, table_sem.at[k])
-        for k, (a, b) in enumerate(((cx_ref, cx), (dx_ref, dx), (coef_ref, coef)))
-    ]
-    arrivals = []
-    for e in range(4):
-        slot, slot_x = places[e][5:]
-        arrivals.append(pltpu.make_async_copy(rims_ref.at[e, slot], mains.at[e], main_sem.at[e]))
-        for k in range(2):
-            arrivals.append(pltpu.make_async_copy(ends_ref.at[e, slot_x + k], exts.at[e, k], ext_sem.at[e, k]))
-    for copy in arrivals + tables + loads:
-        copy.start()
-    for copy in arrivals + tables:
-        copy.wait()
+    end = lambda row, k, line: row[:, 16 * k + line : 16 * k + line + 1]
 
     def ghost(edge, to_ws):
-        on_face, face, partner, flipped, q, slot, slot_x = places[edge]
-        block = mains[edge]
+        block = picked[edge]
         line = [block[k : k + 1, :] for k in range(LINES)]
-        strip = (edge + 2) % 4
-        lo_at, hi_at = {W: (0, 2), S: (0, 1), E: (1, 3), N: (2, 3)}[edge]
-        lo_x = pick(on_face, exts[edge, 0], dx[lo_at, strip])
-        hi_x = pick(on_face, exts[edge, 1], dx[hi_at, strip])
-        first = head(line[5])
+        own, lo_x, hi_x = (block[k : k + 1, :] for k in (9, 10, 11))
+        flipped = block[12:13, 0:1] > 0.5
         lo = dict(
-            s0=end(lo_x, 3, 0), s1=end(lo_x, 3, 1) - G * (first - end(lo_x, 3, 5)),
-            F=end(lo_x, 3, 8), R=end(lo_x, 3, 3), Dn=end(lo_x, 3, 4), Fb=end(lo_x, 2, 8),
+            s0=end(lo_x, 3, 0), s1=end(lo_x, 3, 1) - G * (end(own, 0, 5) - end(lo_x, 3, 5)),
+            F=end(lo_x, 3, 8), R=end(lo_x, 3, 3), Dn=end(lo_x, 3, 4), Fb=end(lo_x, 2, 8), g=end(lo_x, 3, 15),
         )
         hi = dict(
             s0=end(hi_x, 0, 0), s1=end(hi_x, 0, 1) - G * (end(hi_x, 1, 5) - end(hi_x, 0, 5)),
             T0=end(hi_x, 0, 5), Q=end(hi_x, 0, 6), D=end(hi_x, 0, 7), Tb=end(hi_x, 0, 8),
-            F=end(hi_x, 0, 8), R=end(hi_x, 0, 3), Dn=end(hi_x, 0, 4), Fb=end(hi_x, 1, 8),
+            F=end(hi_x, 0, 8), R=end(hi_x, 0, 3), Dn=end(hi_x, 0, 4), Fb=end(hi_x, 1, 8), g=end(hi_x, 0, 15),
         )
-        lo_corner = on_face & (q == 0)
-        hi_corner = on_face & (q == last)
-        safe = lambda x, top: jnp.where(on_face, x, top)
-        g_face, g_edge = safe(face, 0), safe(partner, E if to_ws else W)
-        third_lo = at_corner(g_face, g_edge, True, first)
-        third_hi = at_corner(g_face, g_edge, False, first)
-        for name, value in third_lo.items():
-            lo[name] = pick(lo_corner, value, lo[name])
-        for name, value in third_hi.items():
-            hi[name] = pick(hi_corner, value, hi[name])
-        lo["done"], hi["done"] = lo_corner, hi_corner
-        turned = jnp.dot(block, mirror, precision=lax.Precision.HIGHEST, preferred_element_type=jnp.float32)
-        turned = [turned[k : k + 1, :] for k in range(LINES)]
+        shared = ("s0", "s1", "F", "R", "Dn", "Fb", "g")
+        new_lo = {n: pick(flipped, hi[n], lo[n]) for n in shared}
+        new_hi = {n: pick(flipped, lo[n], hi[n]) for n in shared}
         along = {5: ("T0", -1.0), 6: ("Q", -1.0), 7: ("D", 1.0)}
         if to_ws:
             along[8] = ("Tb", -1.0)
-        out = []
-        for k in range(LINES):
-            if k in along:
-                name, sign = along[k]
-                other = sign * down_by(turned[k], hi[name])
-            else:
-                other = turned[k]
-            out.append(pick(flipped, other, line[k]))
-        new_lo = {n: pick(flipped, hi[n], lo[n]) for n in ("s0", "s1", "F", "R", "Dn", "Fb")}
-        new_hi = {n: pick(flipped, lo[n], hi[n]) for n in ("s0", "s1", "F", "R", "Dn", "Fb")}
         for k, (name, sign) in along.items():
-            new_hi[name] = pick(flipped, sign * head(line[k]), hi[name])
-        new_lo["done"] = jnp.where(flipped, hi_corner, lo_corner)
-        new_hi["done"] = jnp.where(flipped, lo_corner, hi_corner)
-        return out, new_lo, new_hi
+            line[k] = pick((lane == 0) & flipped, sign * hi[name], line[k])
+            new_hi[name] = pick(flipped, sign * end(own, 0, k), hi[name])
+        return line, new_lo, new_hi
 
     (wl, w_lo, w_hi), (sl, s_lo, s_hi) = ghost(W, True), ghost(S, True)
     (el, e_lo, e_hi), (nl, n_lo, n_hi) = ghost(E, False), ghost(N, False)
 
     for d, x in ((w_lo, sl), (w_hi, nl), (s_lo, wl), (s_hi, el)):
-        d["s1"] = pick(d["done"], d["s1"], d["s1"] - G * head(x[5]))
+        d["s1"] = d["s1"] - d["g"] * head(x[5])
 
     west, south, east, north = c == 0, r == 0, c == last, r == last
     take_w, take_s = west & ~south, south & ~west
@@ -596,9 +565,7 @@
     rim_e, rim_n = FluxRim(el, e_lo, e_hi), FluxRim(nl, n_lo, n_hi)
     as_row = lambda col: jnp.sum(jnp.where(diagonal, col, 0.0), axis=0, keepdims=True)
     as_col = lambda row: jnp.sum(jnp.where(diagonal, row, 0.0), axis=1, keepdims=True)
-    for copy in loads:
-        copy.wait()
-    sp_, s_, up_, u_, vp_, v_, dw_, ds_ = (held[k] for k in range(8))
+    sp_, s_, up_, u_, vp_, v_, dw_, ds_ = (x[...] for x in fields)
     first_col, last_col = cols == 0, cols == side - 1
     first_row, last_row = rows == 0, rows == side - 1
     flux_w = flux_s = height_e = height_n = None
@@ -645,57 +612,47 @@
         f32 = jnp.float32
         shape = lambda *dims: jax.ShapeDtypeStruct(dims, f32)
         hbm = pl.BlockSpec(memory_space=pl.ANY)
-        smem = pl.BlockSpec(memory_space=pltpu.SMEM)
+        vmem = pl.BlockSpec(memory_space=pltpu.VMEM)
         dma = pltpu.SemaphoreType.DMA
+        scratch = lambda *dims: pltpu.VMEM(dims, f32)
+        pairs = faces // 2
         links = jnp.transpose(links, (2, 1, 0))
+        fields = (sp, s, up, u, vp, v, dw, ds)
+        grant = 8 << 20
+        in_hbm = [pltpu.with_memory_space_constraint(a, pltpu.HBM) for a in (links, ph, *fields)]
         got = pl.pallas_call(
             functools.partial(exchange, sides, faces),
-            out_shape=(
-                shape(4, 9, 16, side),
-                shape(4, 16, 1, side),
-                shape(8, faces // 2, 4, 1, side),
-                shape(4, 4, 1, side),
-                shape(2 * CONSTITUENTS, side),
-            ),
-            in_specs=[smem] * 2 + [hbm] * 8,
-            out_specs=(hbm,) * 5,
+            out_shape=(shape(4, 16, side), shape(2 * CONSTITUENTS, side)),
+            in_specs=[hbm] * 10,
+            out_specs=(vmem,) * 2,
             scratch_shapes=[
-                pltpu.VMEM((8, side, side), f32),
-                pltpu.VMEM((4, 16, side), f32),
-                pltpu.VMEM((4, 1, side), f32),
-                pltpu.VMEM((4, faces // 2, 16, side), f32),
-                pltpu.VMEM((faces // 2, 4, 1, side), f32),
-                pltpu.VMEM((4, 4, 16, side), f32),
-                pltpu.VMEM((2 * CONSTITUENTS, side), f32),
-                dma((8,)), dma((1,)), dma((4,)), dma((4,)), dma((4,)), dma((4,)),
-                dma((4, faces // 2)), dma((4, faces // 2)), dma((faces // 2,)), dma((faces // 2,)),
+                pltpu.SMEM(links.shape, jnp.int32),
+                pltpu.SMEM(ph.shape, f32),
+                scratch(4, 9, 16, side),
+                scratch(4, 16, 1, side),
+                scratch(8, pairs, 4, 1, side),
+                scratch(4, 4, 1, side),
+                scratch(8, side, side),
+                scratch(4, 2, 16, side),
+                scratch(4, 1, side),
+                scratch(4, pairs, 2, 16, side),
+                scratch(pairs, 4, 1, side),
+                scratch(4, 4, 16, side),
+                dma((8,)), dma((2,)), dma((4,)), dma((4,)), dma((4,)), dma((4,)),
+                dma((4, pairs)), dma((4, pairs)), dma((pairs,)), dma((pairs,)),
                 dma((4,)), dma((4,)), dma((4,)), dma((4,)), dma((1,)), dma((1,)),
             ],
-            compiler_params=pltpu.CompilerParams(collective_id=0, has_side_effects=True),
-        )(links, ph, sp, s, up, u, vp, v, dw, ds)
+            compiler_params=pltpu.CompilerParams(collective_id=0, has_side_effects=True, vmem_limit_bytes=grant),
+        )(*in_hbm)
         tile = shape(side, side)
         return pl.pallas_call(
-            functools.partial(substeps, sides, faces),
+            functools.partial(substeps, sides),
             out_shape=(tile, tile, tile, shape(2 * CONSTITUENTS, side, side)),
-            in_specs=[smem] + [hbm] * 13,
+            in_specs=[vmem] * 10,
             out_specs=(hbm,) * 4,
-            scratch_shapes=[
-                pltpu.VMEM((8, side, side), f32),
-                pltpu.VMEM((4, 16, side), f32),
-                pltpu.VMEM((4, 2, 1, side), f32),
-                pltpu.VMEM((8, faces // 2, 4, 1, side), f32),
-                pltpu.VMEM((4, 4, 1, side), f32),
-                pltpu.VMEM((2 * CONSTITUENTS, side), f32),
-                pltpu.VMEM((3, side, side), f32),
-                pltpu.VMEM((2 * CONSTITUENTS, side, side), f32),
-                dma((8,)),
-                dma((4,)),
-                dma((4, 2)),
-                dma((3,)),
-                dma((3,)),
-                dma((2 * CONSTITUENTS,)),
-            ],
-        )(links, sp, s, up, u, vp, v, dw, ds, *got)
+            scratch_shapes=[scratch(3, side, side), scratch(2 * CONSTITUENTS, side, side), dma((3,)), dma((2 * CONSTITUENTS,))],
+            compiler_params=pltpu.CompilerParams(vmem_limit_bytes=grant),
+        )(*got, *fields)
 
     tiles = P("wide", "narrow")
     return jax.shard_map(

time: 36.8 us -> 33.9 us (0.921)
  Pallas kernels: 35.9 us -> 32.9 us
    pallas_call x1, Pallas kernels: 5.56 us -> 2.74 us  [body(): pl.pallas_call(functools.partial(substeps, sides), out_shape=(tile, tile,...]
where the time goes in v3:
time: 33.9 us; the launch traced here: 33.7 us
  Pallas kernels  32.9 us (97%)
  between operations  0.77 us (2%)
    pallas_call x1, Pallas kernels, body(): pl.pallas_call(functools.partial(exchange, sides, faces), out_shape=(shap...  30.1 us
    pallas_call x1, Pallas kernels, body(): pl.pallas_call(functools.partial(substeps, sides), out_shape=(tile, tile,...  2.74 us

profile of v3, /device:TPU:1, one launch (start us, length us, event | category | flops | bytes accessed | tf_op | source)
XLA Modules:
  0.0 33.7 jit_solution(18223778674891858338)
XLA Ops:
  0.6 0.0 copy-start
  0.6 0.0 copy-start.1
  0.7 0.0 copy-start.2
  0.7 0.0 copy-start.3
  0.7 0.0 copy-start.4
  0.7 0.0 copy-start.5
  0.7 0.0 copy-start.6
  0.7 0.0 copy-start.7
  0.7 30.1 %shard_map.129 = (f32[4,16,128]{2,1,0:T(8,128)S(1)}, f32[16,128]{1,0:T(8,128)S(1)}) custom-call(s32[3,4,8]{2,1,0:T(4,128)} %bitcast.1, f32[8]{0:T(128)} %ph_ref.1, f32[128,128]{1,0:T(8,128)} %refs_0_.3, f32[128,128]{1,0:T(8,128)} %refs_1_.3, f32[128,128]{1,0:T(8,128)} %refs_2_.3, f32[128,128]{1,0:T(8,128)} %refs_3_.3, f32[128,128]{1,0:T(8,128)} %refs_4_.3, ...), custom_call_target="tpu_custom_call" | custom-call | tf_op jit(solution)/shard_map/pallas_call | solution.py:623
  30.8 0.0 copy-done
  30.9 0.0 copy-done.1
  30.9 0.0 copy-done.2
  30.9 0.0 copy-done.3
  30.9 0.0 copy-done.4
  30.9 0.0 copy-done.5
  30.9 0.0 copy-done.6
  30.9 0.0 copy-done.7
  30.9 2.7 %shard_map.130 = (f32[128,128]{1,0:T(8,128)}, f32[128,128]{1,0:T(8,128)}, f32[128,128]{1,0:T(8,128)}, f32[16,128,128]{2,1,0:T(8,128)}) custom-call(f32[4,16,128]{2,1,0:T(8,128)S(1)} %get-tuple-element.6.picked, f32[16,128]{1,0:T(8,128)S(1)} %get-tuple-element.7.coef, f32[128,128]{1,0:T(8,128)S(1)} %copy-done, f32[128,128]{1,0:T(8,128)S(1)} %copy-done.1, ...), custom_call_target="tpu_custom_call" | custom-call | tf_op jit(solution)/shard_map/pallas_call | solution.py:648
Async XLA Ops:
  0.6 30.2 %copy-start = (f32[128,128]{1,0:T(8,128)S(1)}, f32[128,128]{1,0:T(8,128)}, u32[]{:S(2)}) copy-start(f32[128,128]{1,0:T(8,128)} %refs_0_.3) | copy-start | bytes 196612
  0.6 30.2 %copy-start.1 = (f32[128,128]{1,0:T(8,128)S(1)}, f32[128,128]{1,0:T(8,128)}, u32[]{:S(2)}) copy-start(f32[128,128]{1,0:T(8,128)} %refs_1_.3) | copy-start | bytes 196612
  0.7 30.2 %copy-start.2 = (f32[128,128]{1,0:T(8,128)S(1)}, f32[128,128]{1,0:T(8,128)}, u32[]{:S(2)}) copy-start(f32[128,128]{1,0:T(8,128)} %refs_2_.3) | copy-start | bytes 196612
  0.7 30.2 %copy-start.3 = (f32[128,128]{1,0:T(8,128)S(1)}, f32[128,128]{1,0:T(8,128)}, u32[]{:S(2)}) copy-start(f32[128,128]{1,0:T(8,128)} %refs_3_.3) | copy-start | bytes 196612
  0.7 30.2 %copy-start.4 = (f32[128,128]{1,0:T(8,128)S(1)}, f32[128,128]{1,0:T(8,128)}, u32[]{:S(2)}) copy-start(f32[128,128]{1,0:T(8,128)} %refs_4_.3) | copy-start | bytes 196612
  0.7 30.2 %copy-start.5 = (f32[128,128]{1,0:T(8,128)S(1)}, f32[128,128]{1,0:T(8,128)}, u32[]{:S(2)}) copy-start(f32[128,128]{1,0:T(8,128)} %refs_5_.3) | copy-start | bytes 196612
  0.7 30.2 %copy-start.6 = (f32[128,128]{1,0:T(8,128)S(1)}, f32[128,128]{1,0:T(8,128)}, u32[]{:S(2)}) copy-start(f32[128,128]{1,0:T(8,128)} %refs_6_.3) | copy-start | bytes 196612
  0.7 30.2 %copy-start.7 = (f32[128,128]{1,0:T(8,128)S(1)}, f32[128,128]{1,0:T(8,128)}, u32[]{:S(2)}) copy-start(f32[128,128]{1,0:T(8,128)} %refs_7_.3) | copy-start | bytes 196612

commit v4 on v3

--- a/solution.py
+++ b/solution.py
@@ -192,8 +192,8 @@
                 moved = pltpu.roll(moved, by, 1)
             gathered = jnp.where((lane >= 16 * k) & (lane < 16 * k + 16), moved, gathered)
         ends[e] = gathered
-        for k in range(2):
-            pack[e, k, LINES : LINES + 1, :] = gathered
+        pack[e, 0, LINES : LINES + 1, :] = gathered
+        pack[e, 1, LINES : LINES + 1, :] = gathered
     total = lax.broadcasted_iota(jnp.int32, (side, side), 0) + lax.broadcasted_iota(jnp.int32, (side, side), 1)
     mirror = (total == side - 1).astype(jnp.float32)
     turned = jnp.dot(whole, mirror, precision=lax.Precision.HIGHEST, preferred_element_type=jnp.float32)
@@ -203,7 +203,7 @@
             if k in (5, 6, 7) or (k == 8 and e in (E, N)):
                 line_k = jnp.where(lane == 0, 0.0, pltpu.roll(line_k, 1, 1))
                 line_k = line_k if k == 7 else -line_k
-            pack[e, 1, k : k + 1, :] = line_k
+            pack[e, 1, k : k + 1, :] = jnp.where(links[2, e, f] == 1, line_k, pack[e, 0, k : k + 1, :])
 
     pl.semaphore_wait(bar, awaited)
 
@@ -214,7 +214,7 @@
         a, b, ss, rs, device_id=d, device_id_type=MESH
     )
     ring_copies = lambda e: [
-        remote(pack.at[e, :, full], ring.at[e, k, :, full], ring_send.at[e, k], ring_recv.at[e, k], ring_at(k))
+        remote(pack.at[e, 1, full], ring.at[e, k, full], ring_send.at[e, k], ring_recv.at[e, k], ring_at(k))
         for k in range(1, pairs)
     ]
     ends_copies = lambda: [
@@ -264,10 +264,10 @@
 
         @pl.when(has)
         def _(e=e, q=q, line=line, kind=kind, lines=lines):
-            ring[e, 0] = pack[e]
+            ring[e, 0] = pack[e, 1]
             for j, (h, to) in enumerate(lines):
                 far_x = links[0, to, x * 2 + h] // 2
-                chosen[e, j] = ring[e, lax.rem(x - far_x + pairs, pairs), links[2, to, x * 2 + h]]
+                chosen[e, j] = ring[e, lax.rem(x - far_x + pairs, pairs)]
             for j, (h, to) in enumerate(lines):
                 g = x * 2 + h
                 place = lambda p, to=to: (p, line) if to in (W, E) else (line, p)
@@ -317,6 +317,47 @@
     take = lambda ref, ss, rs: remote(ref, ref, ss, rs, here)
     for e, to, dr, dc in near:
 
+        @pl.when(inside(r + dr, c + dc))
+        def _(e=e, to=to, dr=dr, dc=dc):
+            near_copy(e, to, dr, dc).wait_send()
+
+    for k, dr, dc in diagonal:
+
+        @pl.when(inside(r + dr, c + dc))
+        def _(k=k, dr=dr, dc=dc):
+            diag_copy(k, dr, dc).wait_send()
+
+    for e, has, q, line in edges:
+
+        @pl.when(has)
+        def _(e=e, q=q):
+            for copy in ring_copies(e):
+                copy.wait_send()
+
+            @pl.when(~own)
+            def _():
+                take(rims_ref.at[e, pl.ds(0, 8), block], main_send.at[e], main_recv.at[e]).wait_send()
+
+            @pl.when(own)
+            def _():
+                take(rims_ref.at[e, pl.ds(0, 7), block], main_send.at[e], main_recv.at[e]).wait_send()
+
+            @pl.when(is_end(q))
+            def _():
+                take(ends_ref.at[e, pl.ds(0, 8)], ext_send.at[e], ext_recv.at[e]).wait_send()
+
+            @pl.when(~is_end(q))
+            def _():
+                take(ends_ref.at[e], ext_send.at[e], ext_recv.at[e]).wait_send()
+
+    @pl.when(corner)
+    def _():
+        for copy in ends_copies():
+            copy.wait_send()
+        take(table_ref.at[pl.ds(0, 7)], corner_send.at[0], corner_recv.at[0]).wait_send()
+
+    for e, to, dr, dc in near:
+
         @pl.when(inside(r - dr, c - dc))
         def _(e=e, to=to):
             take(rims_ref.at[to, 8, block], near_send.at[e], near_recv.at[e]).wait_recv()
@@ -326,24 +367,6 @@
         @pl.when(inside(r - dr, c - dc))
         def _(k=k):
             take(diag_ref.at[k], diag_send.at[k], diag_recv.at[k]).wait_recv()
-
-    for e, has, q, line in edges:
-
-        @pl.when(has)
-        def _(e=e, q=q):
-            take(rims_ref.at[e, pl.ds(0, 8), block], main_send.at[0], main_recv.at[e]).wait_recv()
-
-            @pl.when(is_end(q))
-            def _():
-                take(ends_ref.at[e, pl.ds(0, 8)], ext_send.at[0], ext_recv.at[e]).wait_recv()
-
-            @pl.when(~is_end(q))
-            def _():
-                take(ends_ref.at[e], ext_send.at[0], ext_recv.at[e]).wait_recv()
-
-    @pl.when(corner)
-    def _():
-        take(table_ref, corner_send.at[0], corner_recv.at[0]).wait_recv()
 
     link = lambda face, edge, k: links[k, edge, face]
     end = lambda row, k, line: row[:, 16 * k + line : 16 * k + line + 1]
@@ -382,6 +405,7 @@
             made = jnp.where(lane == 16 * k + line, value, made)
         return made
 
+    choices = []
     for e, on_face, seg, _ in edges:
         to_ws = e in (W, S)
         across = e in (W, E)
@@ -392,57 +416,37 @@
         slot_x = jnp.where(on_face, (face % 2 * 2 + kind) * 4 + 2 * turn, 0)
         strip = (e + 2) % 4
         lo_at, hi_at = {W: (0, 2), S: (0, 1), E: (1, 3), N: (2, 3)}[e]
-        picked[e] = rims_ref[e, slot]
+        flag = jnp.where(on_face, turn, 0).astype(jnp.float32)
+        picked[e, 12:13, :] = jnp.zeros((1, side), jnp.float32) + flag
+        choices.append((e, on_face, face, partner, q, slot, slot_x, strip, lo_at, hi_at))
+
+    for e, has, q, line in edges:
+
+        @pl.when(has)
+        def _(e=e, q=q):
+            take(rims_ref.at[e, pl.ds(0, 8), block], main_send.at[0], main_recv.at[e]).wait_recv()
+
+            @pl.when(is_end(q))
+            def _():
+                take(ends_ref.at[e, pl.ds(0, 8)], ext_send.at[0], ext_recv.at[e]).wait_recv()
+
+            @pl.when(~is_end(q))
+            def _():
+                take(ends_ref.at[e], ext_send.at[0], ext_recv.at[e]).wait_recv()
+
+    @pl.when(corner)
+    def _():
+        take(table_ref, corner_send.at[0], corner_recv.at[0]).wait_recv()
+
+    for e, on_face, face, partner, q, slot, slot_x, strip, lo_at, hi_at in choices:
+        picked[e, 0:10, :] = rims_ref[e, slot, 0:10, :]
         picked[e, 10:11, :] = jnp.where(on_face, ends_ref[e, slot_x], diag_ref[lo_at, strip])
         picked[e, 11:12, :] = jnp.where(on_face, ends_ref[e, slot_x + 1], diag_ref[hi_at, strip])
-        flag = jnp.where(on_face, turn, 0).astype(jnp.float32)
-        picked[e, 12:13, :] = jnp.zeros((1, side), jnp.float32) + flag
 
         @pl.when(corner & on_face)
         def _(e=e, face=face, partner=partner, q=q):
             picked[e, 10:11, :] = jnp.where(q == 0, at_corner(face, partner, True), picked[e, 10:11, :])
             picked[e, 11:12, :] = jnp.where(q == last, at_corner(face, partner, False), picked[e, 11:12, :])
-
-    for e, to, dr, dc in near:
-
-        @pl.when(inside(r + dr, c + dc))
-        def _(e=e, to=to, dr=dr, dc=dc):
-            near_copy(e, to, dr, dc).wait_send()
-
-    for k, dr, dc in diagonal:
-
-        @pl.when(inside(r + dr, c + dc))
-        def _(k=k, dr=dr, dc=dc):
-            diag_copy(k, dr, dc).wait_send()
-
-    for e, has, q, line in edges:
-
-        @pl.when(has)
-        def _(e=e, q=q):
-            for copy in ring_copies(e):
-                copy.wait_send()
-
-            @pl.when(~own)
-            def _():
-                take(rims_ref.at[e, pl.ds(0, 8), block], main_send.at[e], main_recv.at[e]).wait_send()
-
-            @pl.when(own)
-            def _():
-                take(rims_ref.at[e, pl.ds(0, 7), block], main_send.at[e], main_recv.at[e]).wait_send()
-
-            @pl.when(is_end(q))
-            def _():
-                take(ends_ref.at[e, pl.ds(0, 8)], ext_send.at[e], ext_recv.at[e]).wait_send()
-
-            @pl.when(~is_end(q))
-            def _():
-                take(ends_ref.at[e], ext_send.at[e], ext_recv.at[e]).wait_send()
-
-    @pl.when(corner)
-    def _():
-        for copy in ends_copies():
-            copy.wait_send()
-        take(table_ref.at[pl.ds(0, 7)], corner_send.at[0], corner_recv.at[0]).wait_send()
 
 
 def substeps(sides, picked, coef, *refs):
@@ -635,7 +639,7 @@
                 scratch(8, side, side),
                 scratch(4, 2, 16, side),
                 scratch(4, 1, side),
-                scratch(4, pairs, 2, 16, side),
+                scratch(4, pairs, 16, side),
                 scratch(pairs, 4, 1, side),
                 scratch(4, 4, 16, side),
                 dma((8,)), dma((2,)), dma((4,)), dma((4,)), dma((4,)), dma((4,)),

time: 33.9 us -> 33.3 us (0.982)
  Pallas kernels: 32.9 us -> 32.3 us
    pallas_call x1, Pallas kernels: 30.1 us -> 29.6 us  [body(): pl.pallas_call(functools.partial(exchange, sides, faces), out_shape=(shap...]
where the time goes in v4:
time: 33.3 us; the launch traced here: 33.1 us
  Pallas kernels  32.3 us (97%)
  between operations  0.77 us (2%)
    pallas_call x1, Pallas kernels, body(): pl.pallas_call(functools.partial(exchange, sides, faces), out_shape=(shap...  29.6 us
    pallas_call x1, Pallas kernels, body(): pl.pallas_call(functools.partial(substeps, sides), out_shape=(tile, tile,...  2.74 us

profile of v4, /device:TPU:1, one launch (start us, length us, event | category | flops | bytes accessed | tf_op | source)
XLA Modules:
  0.0 33.1 jit_solution(7592649977906448677)
XLA Ops:
  0.6 0.0 copy-start
  0.6 0.0 copy-start.1
  0.7 0.0 copy-start.2
  0.7 0.0 copy-start.3
  0.7 0.0 copy-start.4
  0.7 0.0 copy-start.5
  0.7 0.0 copy-start.6
  0.7 0.0 copy-start.7
  0.7 29.6 %shard_map.129 = (f32[4,16,128]{2,1,0:T(8,128)S(1)}, f32[16,128]{1,0:T(8,128)S(1)}) custom-call(s32[3,4,8]{2,1,0:T(4,128)} %bitcast.1, f32[8]{0:T(128)} %ph_ref.1, f32[128,128]{1,0:T(8,128)} %refs_0_.3, f32[128,128]{1,0:T(8,128)} %refs_1_.3, f32[128,128]{1,0:T(8,128)} %refs_2_.3, f32[128,128]{1,0:T(8,128)} %refs_3_.3, f32[128,128]{1,0:T(8,128)} %refs_4_.3, ...), custom_call_target="tpu_custom_call" | custom-call | tf_op jit(solution)/shard_map/pallas_call | solution.py:627
  30.3 0.0 copy-done
  30.3 0.0 copy-done.1
  30.3 0.0 copy-done.2
  30.3 0.0 copy-done.3
  30.3 0.0 copy-done.4
  30.4 0.0 copy-done.5
  30.4 0.0 copy-done.6
  30.4 0.0 copy-done.7
  30.4 2.7 %shard_map.130 = (f32[128,128]{1,0:T(8,128)}, f32[128,128]{1,0:T(8,128)}, f32[128,128]{1,0:T(8,128)}, f32[16,128,128]{2,1,0:T(8,128)}) custom-call(f32[4,16,128]{2,1,0:T(8,128)S(1)} %get-tuple-element.6.picked, f32[16,128]{1,0:T(8,128)S(1)} %get-tuple-element.7.coef, f32[128,128]{1,0:T(8,128)S(1)} %copy-done, f32[128,128]{1,0:T(8,128)S(1)} %copy-done.1, ...), custom_call_target="tpu_custom_call" | custom-call | tf_op jit(solution)/shard_map/pallas_call | solution.py:652
Async XLA Ops:
  0.6 29.7 %copy-start = (f32[128,128]{1,0:T(8,128)S(1)}, f32[128,128]{1,0:T(8,128)}, u32[]{:S(2)}) copy-start(f32[128,128]{1,0:T(8,128)} %refs_0_.3) | copy-start | bytes 196612
  0.6 29.7 %copy-start.1 = (f32[128,128]{1,0:T(8,128)S(1)}, f32[128,128]{1,0:T(8,128)}, u32[]{:S(2)}) copy-start(f32[128,128]{1,0:T(8,128)} %refs_1_.3) | copy-start | bytes 196612
  0.7 29.7 %copy-start.2 = (f32[128,128]{1,0:T(8,128)S(1)}, f32[128,128]{1,0:T(8,128)}, u32[]{:S(2)}) copy-start(f32[128,128]{1,0:T(8,128)} %refs_2_.3) | copy-start | bytes 196612
  0.7 29.7 %copy-start.3 = (f32[128,128]{1,0:T(8,128)S(1)}, f32[128,128]{1,0:T(8,128)}, u32[]{:S(2)}) copy-start(f32[128,128]{1,0:T(8,128)} %refs_3_.3) | copy-start | bytes 196612
  0.7 29.7 %copy-start.4 = (f32[128,128]{1,0:T(8,128)S(1)}, f32[128,128]{1,0:T(8,128)}, u32[]{:S(2)}) copy-start(f32[128,128]{1,0:T(8,128)} %refs_4_.3) | copy-start | bytes 196612
  0.7 29.7 %copy-start.5 = (f32[128,128]{1,0:T(8,128)S(1)}, f32[128,128]{1,0:T(8,128)}, u32[]{:S(2)}) copy-start(f32[128,128]{1,0:T(8,128)} %refs_5_.3) | copy-start | bytes 196612
  0.7 29.7 %copy-start.6 = (f32[128,128]{1,0:T(8,128)S(1)}, f32[128,128]{1,0:T(8,128)}, u32[]{:S(2)}) copy-start(f32[128,128]{1,0:T(8,128)} %refs_6_.3) | copy-start | bytes 196612
  0.7 29.7 %copy-start.7 = (f32[128,128]{1,0:T(8,128)S(1)}, f32[128,128]{1,0:T(8,128)}, u32[]{:S(2)}) copy-start(f32[128,128]{1,0:T(8,128)} %refs_7_.3) | copy-start | bytes 196612

commit v5 on v4

--- a/solution.py
+++ b/solution.py
@@ -66,12 +66,27 @@
     return low, high
 
 
+def merge(raw, high, lane):
+    up0 = lambda x: jnp.where(lane == lane.shape[1] - 1, 0.0, pltpu.roll(x, lane.shape[1] - 1, 1))
+    down0 = lambda x: jnp.where(lane == 0, 0.0, pltpu.roll(x, 1, 1))
+    s0, y1, y2, a, b, t0, q, d, last_line = raw
+    t1 = q - d * (s0 - down0(s0))
+    if high:
+        older = 0.8 * t0 + 0.1 * q + 0.1 * t1
+        x3 = a - G * (up0(older) - older) - G * b * (G * (up0(last_line) - last_line))
+        return [s0, y1 - G * (up0(t0) - t0), y2 - G * (up0(t1) - t1), x3, b, d]
+    f0, was = last_line, a
+    s1 = y1 - G * (up0(t0) - t0)
+    s2 = y2 + 0.1 * s1 - G * (up0(t1) - t1)
+    return [f0, was - b * s0, 0.8 * f0 + 0.1 * was - b * s1, 0.08 * f0 + 0.01 * was - b * s2, b]
+
+
 def exchange(sides, faces, links_ref, ph_ref, *refs):
     fields, refs = refs[:8], refs[8:]
     (
         picked, coef,
         links, ph, rims_ref, ends_ref, table_ref, diag_ref,
-        held, pack, ends, ring, ring_ends, chosen,
+        held, pack, sent, ends, ring, ring_ends, chosen,
         load_sem, links_sem, near_send, near_recv, diag_send, diag_recv, ring_send, ring_recv, ring_ends_send, ring_ends_recv,
         main_send, main_recv, ext_send, ext_recv, corner_send, corner_recv,
     ) = refs
@@ -170,17 +185,16 @@
     sp, s, up, u, vp, v, dw, ds = (held.at[k] for k in range(8))
     lo, hi = rims(s[...], sp[...], v[...], vp[...], u[...], up[...], ds[...], dw[...])
     for k in range(LINES):
-        pack[S, 0, k : k + 1, :] = lo[k]
-        pack[N, 0, k : k + 1, :] = hi[k]
+        pack[S, k : k + 1, :] = lo[k]
+        pack[N, k : k + 1, :] = hi[k]
     flip = lambda ref: jnp.transpose(ref[...])
     lo, hi = rims(flip(s), flip(sp), flip(u), flip(up), flip(v), flip(vp), flip(dw), flip(ds))
     for k in range(LINES):
-        pack[W, 0, k : k + 1, :] = lo[k]
-        pack[E, 0, k : k + 1, :] = hi[k]
+        pack[W, k : k + 1, :] = lo[k]
+        pack[E, k : k + 1, :] = hi[k]
     for e in range(4):
-        pack[e, 0, LINES:16, :] = jnp.full((16 - LINES, side), G, jnp.float32)
-    whole = jnp.concatenate([pack[e, 0] for e in range(4)], axis=0)
-    stacked = jnp.concatenate([whole, jnp.zeros((side - 64, side), jnp.float32)], axis=0)
+        pack[e, LINES:16, :] = jnp.full((16 - LINES, side), G, jnp.float32)
+    stacked = jnp.concatenate([pack[e] for e in range(4)] + [jnp.zeros((side - 64, side), jnp.float32)], axis=0)
     turned = jnp.transpose(stacked)
     lane = lax.broadcasted_iota(jnp.int32, (1, side), 1)
     for e in range(4):
@@ -192,29 +206,32 @@
                 moved = pltpu.roll(moved, by, 1)
             gathered = jnp.where((lane >= 16 * k) & (lane < 16 * k + 16), moved, gathered)
         ends[e] = gathered
-        pack[e, 0, LINES : LINES + 1, :] = gathered
-        pack[e, 1, LINES : LINES + 1, :] = gathered
+        merged = merge([pack[e, k : k + 1, :] for k in range(LINES)], e in (E, N), lane)
+        for k, line_k in enumerate(merged):
+            sent[e, 0, k : k + 1, :] = line_k
+        for k in range(len(merged), 7):
+            sent[e, 0, k : k + 1, :] = jnp.zeros((1, side), jnp.float32)
+        sent[e, 0, 7:8, :] = gathered
+        sent[e, 1, 7:8, :] = gathered
     total = lax.broadcasted_iota(jnp.int32, (side, side), 0) + lax.broadcasted_iota(jnp.int32, (side, side), 1)
     mirror = (total == side - 1).astype(jnp.float32)
+    whole = jnp.concatenate([sent[e, 0] for e in range(4)], axis=0)
     turned = jnp.dot(whole, mirror, precision=lax.Precision.HIGHEST, preferred_element_type=jnp.float32)
     for e in range(4):
-        for k in range(LINES):
-            line_k = turned[16 * e + k : 16 * e + k + 1, :]
-            if k in (5, 6, 7) or (k == 8 and e in (E, N)):
+        for k in range(7):
+            line_k = turned[8 * e + k : 8 * e + k + 1, :]
+            if k == 5:
                 line_k = jnp.where(lane == 0, 0.0, pltpu.roll(line_k, 1, 1))
-                line_k = line_k if k == 7 else -line_k
-            pack[e, 1, k : k + 1, :] = jnp.where(links[2, e, f] == 1, line_k, pack[e, 0, k : k + 1, :])
+            sent[e, 1, k : k + 1, :] = jnp.where(links[2, e, f] == 1, line_k, sent[e, 0, k : k + 1, :])
 
     pl.semaphore_wait(bar, awaited)
 
-    full = pl.ds(0, LINES + 1)
-    block = full
     here = (w, c)
     remote = lambda a, b, ss, rs, d: pltpu.make_async_remote_copy(
         a, b, ss, rs, device_id=d, device_id_type=MESH
     )
     ring_copies = lambda e: [
-        remote(pack.at[e, 1, full], ring.at[e, k, full], ring_send.at[e, k], ring_recv.at[e, k], ring_at(k))
+        remote(sent.at[e, 1], ring.at[e, k], ring_send.at[e, k], ring_recv.at[e, k], ring_at(k))
         for k in range(1, pairs)
     ]
     ends_copies = lambda: [
@@ -235,7 +252,7 @@
     near = [(E, W, 0, 1), (N, S, 1, 0), (W, E, 0, -1), (S, N, -1, 0)]
     diagonal = [(0, 1, 1), (1, 1, -1), (2, -1, 1), (3, -1, -1)]
     near_copy = lambda e, to, dr, dc: remote(
-        pack.at[e, 0, block], rims_ref.at[to, 8, block], near_send.at[e], near_recv.at[e], at(f, r + dr, c + dc)
+        sent.at[e, 0], rims_ref.at[to, 8], near_send.at[e], near_recv.at[e], at(f, r + dr, c + dc)
     )
     diag_copy = lambda k, dr, dc: remote(ends, diag_ref.at[k], diag_send.at[k], diag_recv.at[k], at(f, r + dr, c + dc))
     for e, to, dr, dc in near:
@@ -264,7 +281,7 @@
 
         @pl.when(has)
         def _(e=e, q=q, line=line, kind=kind, lines=lines):
-            ring[e, 0] = pack[e, 1]
+            ring[e, 0] = sent[e, 1]
             for j, (h, to) in enumerate(lines):
                 far_x = links[0, to, x * 2 + h] // 2
                 chosen[e, j] = ring[e, lax.rem(x - far_x + pairs, pairs)]
@@ -279,12 +296,12 @@
                     @pl.when(~mine)
                     def _(j=j, to=to, slot=slot, g=g, row=row, col=col):
                         remote(
-                            chosen.at[e, j, block], rims_ref.at[to, slot, block], main_send.at[e], main_recv.at[to], at(g, row, col)
+                            chosen.at[e, j], rims_ref.at[to, slot], main_send.at[e], main_recv.at[to], at(g, row, col)
                         ).start()
 
                     @pl.when(mine)
                     def _(j=j, to=to, slot=slot):
-                        pltpu.make_async_copy(chosen.at[e, j, block], rims_ref.at[to, slot, block], main_recv.at[to]).start()
+                        pltpu.make_async_copy(chosen.at[e, j], rims_ref.at[to, slot], main_recv.at[to]).start()
 
             for j, (h, to) in enumerate(lines):
                 g = x * 2 + h
@@ -296,7 +313,7 @@
                     @pl.when((p >= 0) & (p <= last))
                     def _(j=j, to=to, slot=slot, g=g, row=row, col=col):
                         remote(
-                            chosen.at[e, j, pl.ds(LINES, 1)], ends_ref.at[to, slot], ext_send.at[e], ext_recv.at[to], at(g, row, col)
+                            chosen.at[e, j, pl.ds(7, 1)], ends_ref.at[to, slot], ext_send.at[e], ext_recv.at[to], at(g, row, col)
                         ).start()
 
     corner_copy = lambda i: remote(ring_ends, table_ref.at[me_corner], corner_send.at[0], corner_recv.at[0], corner_at(i))
@@ -336,11 +353,11 @@
 
             @pl.when(~own)
             def _():
-                take(rims_ref.at[e, pl.ds(0, 8), block], main_send.at[e], main_recv.at[e]).wait_send()
+                take(rims_ref.at[e, pl.ds(0, 8)], main_send.at[e], main_recv.at[e]).wait_send()
 
             @pl.when(own)
             def _():
-                take(rims_ref.at[e, pl.ds(0, 7), block], main_send.at[e], main_recv.at[e]).wait_send()
+                take(rims_ref.at[e, pl.ds(0, 7)], main_send.at[e], main_recv.at[e]).wait_send()
 
             @pl.when(is_end(q))
             def _():
@@ -360,7 +377,7 @@
 
         @pl.when(inside(r - dr, c - dc))
         def _(e=e, to=to):
-            take(rims_ref.at[to, 8, block], near_send.at[e], near_recv.at[e]).wait_recv()
+            take(rims_ref.at[to, 8], near_send.at[e], near_recv.at[e]).wait_recv()
 
     for k, dr, dc in diagonal:
 
@@ -424,7 +441,7 @@
 
         @pl.when(has)
         def _(e=e, q=q):
-            take(rims_ref.at[e, pl.ds(0, 8), block], main_send.at[0], main_recv.at[e]).wait_recv()
+            take(rims_ref.at[e, pl.ds(0, 8)], main_send.at[0], main_recv.at[e]).wait_recv()
 
             @pl.when(is_end(q))
             def _():
@@ -439,7 +456,7 @@
         take(table_ref, corner_send.at[0], corner_recv.at[0]).wait_recv()
 
     for e, on_face, face, partner, q, slot, slot_x, strip, lo_at, hi_at in choices:
-        picked[e, 0:10, :] = rims_ref[e, slot, 0:10, :]
+        picked[e, 0:8, :] = rims_ref[e, slot]
         picked[e, 10:11, :] = jnp.where(on_face, ends_ref[e, slot_x], diag_ref[lo_at, strip])
         picked[e, 11:12, :] = jnp.where(on_face, ends_ref[e, slot_x + 1], diag_ref[hi_at, strip])
 
@@ -469,8 +486,8 @@
 
     def ghost(edge, to_ws):
         block = picked[edge]
-        line = [block[k : k + 1, :] for k in range(LINES)]
-        own, lo_x, hi_x = (block[k : k + 1, :] for k in (9, 10, 11))
+        line = [block[k : k + 1, :] for k in range(6 if to_ws else 5)]
+        own, lo_x, hi_x = (block[k : k + 1, :] for k in (7, 10, 11))
         flipped = block[12:13, 0:1] > 0.5
         lo = dict(
             s0=end(lo_x, 3, 0), s1=end(lo_x, 3, 1) - G * (end(own, 0, 5) - end(lo_x, 3, 5)),
@@ -484,19 +501,20 @@
         shared = ("s0", "s1", "F", "R", "Dn", "Fb", "g")
         new_lo = {n: pick(flipped, hi[n], lo[n]) for n in shared}
         new_hi = {n: pick(flipped, lo[n], hi[n]) for n in shared}
-        along = {5: ("T0", -1.0), 6: ("Q", -1.0), 7: ("D", 1.0)}
+        for name in ("T0", "Q", "D", "Tb"):
+            new_hi[name] = hi[name]
         if to_ws:
-            along[8] = ("Tb", -1.0)
-        for k, (name, sign) in along.items():
-            line[k] = pick((lane == 0) & flipped, sign * hi[name], line[k])
-            new_hi[name] = pick(flipped, sign * end(own, 0, k), hi[name])
-        return line, new_lo, new_hi
-
-    (wl, w_lo, w_hi), (sl, s_lo, s_hi) = ghost(W, True), ghost(S, True)
-    (el, e_lo, e_hi), (nl, n_lo, n_hi) = ghost(E, False), ghost(N, False)
-
-    for d, x in ((w_lo, sl), (w_hi, nl), (s_lo, wl), (s_hi, el)):
-        d["s1"] = d["s1"] - d["g"] * head(x[5])
+            line[5] = pick((lane == 0) & flipped, hi["D"], line[5])
+            new_hi["D"] = pick(flipped, end(own, 0, 7), hi["D"])
+        new_lo["first"] = pick(flipped, -hi["T0"], end(own, 0, 5))
+        theirs = (flipped, lo, hi, own)
+        return line, new_lo, new_hi, theirs
+
+    (wl, w_lo, w_hi, w_own), (sl, s_lo, s_hi, s_own) = ghost(W, True), ghost(S, True)
+    (el, e_lo, e_hi, e_own), (nl, n_lo, n_hi, n_own) = ghost(E, False), ghost(N, False)
+
+    for d, x in ((w_lo, s_lo), (w_hi, n_lo), (s_lo, w_lo), (s_hi, e_lo)):
+        d["s1"] = d["s1"] - d["g"] * x["first"]
 
     west, south, east, north = c == 0, r == 0, c == last, r == last
     take_w, take_s = west & ~south, south & ~west
@@ -520,53 +538,62 @@
     n_hi.update(ne_n)
     e_hi.update(ne_e)
 
+    def missing(lo, hi, theirs):
+        flipped, their_lo, their_hi, own = theirs
+        place = pick(flipped, side - 1 - lane, lane)
+        t0, q, d, s0 = (pick(flipped, their_hi[n], hi[n]) for n in ("T0", "Q", "D", "s0"))
+        tb = pick(flipped, their_hi["Tb"], hi["Tb"])
+        low = end(own, 0, 7) * pick(flipped, their_lo["s0"], lo["s0"])
+        t1 = q - d * (s0 - end(own, 3, 0))
+        return place == side - 1, place == 0, t0, t1, 0.8 * t0 + 0.1 * q + 0.1 * t1, tb, low
+
     class HeightRim:
-        def __init__(self, line, lo, hi):
-            self.line, self.lo, self.hi = line, lo, hi
+        def __init__(self, line, lo, hi, theirs):
+            top, bottom, t0, t1, t2, tb, low = missing(lo, hi, theirs)
+            s0, x1, x2, x3, back, d = line
+            x1 = x1 - jnp.where(top, G * t0, 0.0)
+            x2 = x2 - jnp.where(top, G * t1, 0.0) + jnp.where(bottom, G * low, 0.0)
+            x3 = x3 - jnp.where(top, G * t2 + G * back * (G * tb), 0.0) + jnp.where(bottom, G * (0.1 * low), 0.0)
+            self.line = s0, x1, x2, x3, back, d
+            self.lo, self.hi = lo, hi
 
         def at(self, n, flux):
-            s0, y1, y2, z, back, t0, q, d, tb = self.line
-            lo, hi = self.lo, self.hi
+            s0, x1, x2, x3, back, d = self.line
             if n == 0:
                 return s0
             if n == 1:
-                self.s1 = y1 - G * flux - G * (up_by(t0, hi["T0"]) - t0)
+                self.s1 = x1 - G * flux
                 return self.s1
+            s1 = self.s1
             if n == 2:
-                self.t1 = q - d * (s0 - down_by(s0, lo["s0"]))
-                self.t1hi = hi["Q"] - hi["D"] * (hi["s0"] - tail(s0))
-                self.s2 = y2 + 0.1 * self.s1 - G * flux - G * (up_by(self.t1, self.t1hi) - self.t1)
+                self.s2 = x2 + 0.1 * s1 - G * flux
                 return self.s2
-            s1 = self.s1
-            t2 = 0.8 * t0 + 0.1 * q + 0.1 * self.t1 - d * (s1 - down_by(s1, lo["s1"]))
-            t2hi = 0.8 * hi["T0"] + 0.1 * hi["Q"] + 0.1 * self.t1hi - hi["D"] * (hi["s1"] - tail(s1))
-            inner = s1 + G * (up_by(tb, hi["Tb"]) - tb)
-            return 0.81 * s1 + 0.1 * self.s2 + z - G * back * inner - G * flux - G * (up_by(t2, t2hi) - t2)
+            slope = d * (s1 - down_by(s1, self.lo["s1"]))
+            slope_hi = self.hi["D"] * (self.hi["s1"] - tail(s1))
+            return x3 + 0.81 * s1 + 0.1 * self.s2 - G * back * s1 - G * flux + G * (up_by(slope, slope_hi) - slope)
 
     class FluxRim:
-        def __init__(self, line, lo, hi):
-            self.line, self.lo, self.hi = line, lo, hi
+        def __init__(self, line, lo, hi, theirs):
+            top, bottom, t0, t1, _, _, low = missing(lo, hi, theirs)
+            f0, p1, p2, p3, d = line
+            p2 = p2 + d * jnp.where(top, G * t0, 0.0)
+            p3 = p3 + d * (jnp.where(top, G * (0.1 * t0 + t1), 0.0) - jnp.where(bottom, G * low, 0.0))
+            self.line = f0, p1, p2, p3, d
 
         def at(self, n, height):
-            s0, u1, u2, r_, d_, t0, q, d, f0 = self.line
-            lo, hi = self.lo, self.hi
+            f0, p1, p2, p3, d = self.line
             if n == 0:
                 return f0
             if n == 1:
-                self.f1 = r_ - d_ * (s0 - height)
+                self.f1 = p1 + d * height
                 return self.f1
             if n == 2:
-                self.s1 = u1 - G * (up_by(t0, hi["T0"]) - t0)
-                self.older = 0.8 * f0 + 0.1 * r_ + 0.1 * self.f1
-                self.f2 = self.older - d_ * (self.s1 - height)
+                self.f2 = p2 + 0.1 * self.f1 + d * height
                 return self.f2
-            t1 = q - d * (s0 - down_by(s0, lo["s0"]))
-            t1hi = hi["Q"] - hi["D"] * (hi["s0"] - tail(s0))
-            s2 = u2 + 0.1 * self.s1 + G * self.f1 - G * (up_by(t1, t1hi) - t1)
-            return 0.8 * self.f1 + 0.1 * self.f2 + 0.1 * self.older - d_ * (s2 - height)
-
-    rim_w, rim_s = HeightRim(wl, w_lo, w_hi), HeightRim(sl, s_lo, s_hi)
-    rim_e, rim_n = FluxRim(el, e_lo, e_hi), FluxRim(nl, n_lo, n_hi)
+            return p3 + (0.81 - G * d) * self.f1 + 0.1 * self.f2 + d * height
+
+    rim_w, rim_s = HeightRim(wl, w_lo, w_hi, w_own), HeightRim(sl, s_lo, s_hi, s_own)
+    rim_e, rim_n = FluxRim(el, e_lo, e_hi, e_own), FluxRim(nl, n_lo, n_hi, n_own)
     as_row = lambda col: jnp.sum(jnp.where(diagonal, col, 0.0), axis=0, keepdims=True)
     as_col = lambda row: jnp.sum(jnp.where(diagonal, row, 0.0), axis=1, keepdims=True)
     sp_, s_, up_, u_, vp_, v_, dw_, ds_ = (x[...] for x in fields)
@@ -632,16 +659,17 @@
             scratch_shapes=[
                 pltpu.SMEM(links.shape, jnp.int32),
                 pltpu.SMEM(ph.shape, f32),
-                scratch(4, 9, 16, side),
+                scratch(4, 9, 8, side),
                 scratch(4, 16, 1, side),
                 scratch(8, pairs, 4, 1, side),
                 scratch(4, 4, 1, side),
                 scratch(8, side, side),
-                scratch(4, 2, 16, side),
+                scratch(4, 16, side),
+                scratch(4, 2, 8, side),
                 scratch(4, 1, side),
-                scratch(4, pairs, 16, side),
+                scratch(4, pairs, 8, side),
                 scratch(pairs, 4, 1, side),
-                scratch(4, 4, 16, side),
+                scratch(4, 4, 8, side),
                 dma((8,)), dma((2,)), dma((4,)), dma((4,)), dma((4,)), dma((4,)),
                 dma((4, pairs)), dma((4, pairs)), dma((pairs,)), dma((pairs,)),
                 dma((4,)), dma((4,)), dma((4,)), dma((4,)), dma((1,)), dma((1,)),

time: 33.3 us -> 33 us (level)
  no operation moved by 1% of the time
where the time goes in v5:
time: 33 us; the launch traced here: 32.8 us
  Pallas kernels  32 us (97%)
  between operations  0.77 us (2%)
    pallas_call x1, Pallas kernels, body(): pl.pallas_call(functools.partial(exchange, sides, faces), out_shape=(shap...  29.5 us
    pallas_call x1, Pallas kernels, body(): pl.pallas_call(functools.partial(substeps, sides), out_shape=(tile, tile,...  2.53 us

profile of v5, /device:TPU:1, one launch (start us, length us, event | category | flops | bytes accessed | tf_op | source)
XLA Modules:
  0.0 32.8 jit_solution(12635402365297728452)
XLA Ops:
  0.6 0.0 copy-start
  0.6 0.0 copy-start.1
  0.7 0.0 copy-start.2
  0.7 0.0 copy-start.3
  0.7 0.0 copy-start.4
  0.7 0.0 copy-start.5
  0.7 0.0 copy-start.6
  0.7 0.0 copy-start.7
  0.7 29.5 %shard_map.129 = (f32[4,16,128]{2,1,0:T(8,128)S(1)}, f32[16,128]{1,0:T(8,128)S(1)}) custom-call(s32[3,4,8]{2,1,0:T(4,128)} %bitcast.1, f32[8]{0:T(128)} %ph_ref.1, f32[128,128]{1,0:T(8,128)} %refs_0_.3, f32[128,128]{1,0:T(8,128)} %refs_1_.3, f32[128,128]{1,0:T(8,128)} %refs_2_.3, f32[128,128]{1,0:T(8,128)} %refs_3_.3, f32[128,128]{1,0:T(8,128)} %refs_4_.3, ...), custom_call_target="tpu_custom_call" | custom-call | tf_op jit(solution)/shard_map/pallas_call | solution.py:654
  30.2 0.0 copy-done
  30.2 0.0 copy-done.1
  30.2 0.0 copy-done.2
  30.2 0.0 copy-done.3
  30.2 0.0 copy-done.4
  30.2 0.0 copy-done.5
  30.2 0.0 copy-done.6
  30.3 0.0 copy-done.7
  30.3 2.5 %shard_map.130 = (f32[128,128]{1,0:T(8,128)}, f32[128,128]{1,0:T(8,128)}, f32[128,128]{1,0:T(8,128)}, f32[16,128,128]{2,1,0:T(8,128)}) custom-call(f32[4,16,128]{2,1,0:T(8,128)S(1)} %get-tuple-element.6.picked, f32[16,128]{1,0:T(8,128)S(1)} %get-tuple-element.7.coef, f32[128,128]{1,0:T(8,128)S(1)} %copy-done, f32[128,128]{1,0:T(8,128)S(1)} %copy-done.1, ...), custom_call_target="tpu_custom_call" | custom-call | tf_op jit(solution)/shard_map/pallas_call | solution.py:680
Async XLA Ops:
  0.6 29.6 %copy-start = (f32[128,128]{1,0:T(8,128)S(1)}, f32[128,128]{1,0:T(8,128)}, u32[]{:S(2)}) copy-start(f32[128,128]{1,0:T(8,128)} %refs_0_.3) | copy-start | bytes 196612
  0.6 29.6 %copy-start.1 = (f32[128,128]{1,0:T(8,128)S(1)}, f32[128,128]{1,0:T(8,128)}, u32[]{:S(2)}) copy-start(f32[128,128]{1,0:T(8,128)} %refs_1_.3) | copy-start | bytes 196612
  0.7 29.6 %copy-start.2 = (f32[128,128]{1,0:T(8,128)S(1)}, f32[128,128]{1,0:T(8,128)}, u32[]{:S(2)}) copy-start(f32[128,128]{1,0:T(8,128)} %refs_2_.3) | copy-start | bytes 196612
  0.7 29.6 %copy-start.3 = (f32[128,128]{1,0:T(8,128)S(1)}, f32[128,128]{1,0:T(8,128)}, u32[]{:S(2)}) copy-start(f32[128,128]{1,0:T(8,128)} %refs_3_.3) | copy-start | bytes 196612
  0.7 29.6 %copy-start.4 = (f32[128,128]{1,0:T(8,128)S(1)}, f32[128,128]{1,0:T(8,128)}, u32[]{:S(2)}) copy-start(f32[128,128]{1,0:T(8,128)} %refs_4_.3) | copy-start | bytes 196612
  0.7 29.6 %copy-start.5 = (f32[128,128]{1,0:T(8,128)S(1)}, f32[128,128]{1,0:T(8,128)}, u32[]{:S(2)}) copy-start(f32[128,128]{1,0:T(8,128)} %refs_5_.3) | copy-start | bytes 196612
  0.7 29.6 %copy-start.6 = (f32[128,128]{1,0:T(8,128)S(1)}, f32[128,128]{1,0:T(8,128)}, u32[]{:S(2)}) copy-start(f32[128,128]{1,0:T(8,128)} %refs_6_.3) | copy-start | bytes 196612
  0.7 29.6 %copy-start.7 = (f32[128,128]{1,0:T(8,128)S(1)}, f32[128,128]{1,0:T(8,128)}, u32[]{:S(2)}) copy-start(f32[128,128]{1,0:T(8,128)} %refs_7_.3) | copy-start | bytes 196612

commit v6 on v5

--- a/solution.py
+++ b/solution.py
@@ -288,6 +288,19 @@
             for j, (h, to) in enumerate(lines):
                 g = x * 2 + h
                 place = lambda p, to=to: (p, line) if to in (W, E) else (line, p)
+                for kind_x, p in enumerate(ext_to(q)):
+                    slot = (half * 2 + kind) * 4 + kind_x
+                    row, col = place(p)
+
+                    @pl.when((p >= 0) & (p <= last))
+                    def _(j=j, to=to, slot=slot, g=g, row=row, col=col):
+                        remote(
+                            chosen.at[e, j, pl.ds(7, 1)], ends_ref.at[to, slot], ext_send.at[e], ext_recv.at[to], at(g, row, col)
+                        ).start()
+
+            for j, (h, to) in enumerate(lines):
+                g = x * 2 + h
+                place = lambda p, to=to: (p, line) if to in (W, E) else (line, p)
                 for par, p in enumerate((q, last - q)):
                     slot = (half * 2 + kind) * 2 + par
                     row, col = place(p)
@@ -302,19 +315,6 @@
                     @pl.when(mine)
                     def _(j=j, to=to, slot=slot):
                         pltpu.make_async_copy(chosen.at[e, j], rims_ref.at[to, slot], main_recv.at[to]).start()
-
-            for j, (h, to) in enumerate(lines):
-                g = x * 2 + h
-                place = lambda p, to=to: (p, line) if to in (W, E) else (line, p)
-                for kind_x, p in enumerate(ext_to(q)):
-                    slot = (half * 2 + kind) * 4 + kind_x
-                    row, col = place(p)
-
-                    @pl.when((p >= 0) & (p <= last))
-                    def _(j=j, to=to, slot=slot, g=g, row=row, col=col):
-                        remote(
-                            chosen.at[e, j, pl.ds(7, 1)], ends_ref.at[to, slot], ext_send.at[e], ext_recv.at[to], at(g, row, col)
-                        ).start()
 
     corner_copy = lambda i: remote(ring_ends, table_ref.at[me_corner], corner_send.at[0], corner_recv.at[0], corner_at(i))
 

time: 33 us -> 32.6 us (0.988)
  Pallas kernels: 32 us -> 31.6 us
    pallas_call x1, Pallas kernels: 29.5 us -> 29.1 us  [body(): pl.pallas_call(functools.partial(exchange, sides, faces), out_shape=(shap...]
where the time goes in v6:
time: 32.6 us; the launch traced here: 32.4 us
  Pallas kernels  31.6 us (97%)
  between operations  0.77 us (2%)
    pallas_call x1, Pallas kernels, body(): pl.pallas_call(functools.partial(exchange, sides, faces), out_shape=(shap...  29.1 us
    pallas_call x1, Pallas kernels, body(): pl.pallas_call(functools.partial(substeps, sides), out_shape=(tile, tile,...  2.53 us

profile of v6, /device:TPU:1, one launch (start us, length us, event | category | flops | bytes accessed | tf_op | source)
XLA Modules:
  0.0 32.4 jit_solution(2261972627930328213)
XLA Ops:
  0.6 0.0 copy-start
  0.6 0.0 copy-start.1
  0.7 0.0 copy-start.2
  0.7 0.0 copy-start.3
  0.7 0.0 copy-start.4
  0.7 0.0 copy-start.5
  0.7 0.0 copy-start.6
  0.7 0.0 copy-start.7
  0.7 29.1 %shard_map.129 = (f32[4,16,128]{2,1,0:T(8,128)S(1)}, f32[16,128]{1,0:T(8,128)S(1)}) custom-call(s32[3,4,8]{2,1,0:T(4,128)} %bitcast.1, f32[8]{0:T(128)} %ph_ref.1, f32[128,128]{1,0:T(8,128)} %refs_0_.3, f32[128,128]{1,0:T(8,128)} %refs_1_.3, f32[128,128]{1,0:T(8,128)} %refs_2_.3, f32[128,128]{1,0:T(8,128)} %refs_3_.3, f32[128,128]{1,0:T(8,128)} %refs_4_.3, ...), custom_call_target="tpu_custom_call" | custom-call | tf_op jit(solution)/shard_map/pallas_call | solution.py:654
  29.8 0.0 copy-done
  29.8 0.0 copy-done.1
  29.8 0.0 copy-done.2
  29.8 0.0 copy-done.3
  29.8 0.0 copy-done.4
  29.8 0.0 copy-done.5
  29.9 0.0 copy-done.6
  29.9 0.0 copy-done.7
  29.9 2.5 %shard_map.130 = (f32[128,128]{1,0:T(8,128)}, f32[128,128]{1,0:T(8,128)}, f32[128,128]{1,0:T(8,128)}, f32[16,128,128]{2,1,0:T(8,128)}) custom-call(f32[4,16,128]{2,1,0:T(8,128)S(1)} %get-tuple-element.6.picked, f32[16,128]{1,0:T(8,128)S(1)} %get-tuple-element.7.coef, f32[128,128]{1,0:T(8,128)S(1)} %copy-done, f32[128,128]{1,0:T(8,128)S(1)} %copy-done.1, ...), custom_call_target="tpu_custom_call" | custom-call | tf_op jit(solution)/shard_map/pallas_call | solution.py:680
Async XLA Ops:
  0.6 29.2 %copy-start = (f32[128,128]{1,0:T(8,128)S(1)}, f32[128,128]{1,0:T(8,128)}, u32[]{:S(2)}) copy-start(f32[128,128]{1,0:T(8,128)} %refs_0_.3) | copy-start | bytes 196612
  0.6 29.2 %copy-start.1 = (f32[128,128]{1,0:T(8,128)S(1)}, f32[128,128]{1,0:T(8,128)}, u32[]{:S(2)}) copy-start(f32[128,128]{1,0:T(8,128)} %refs_1_.3) | copy-start | bytes 196612
  0.7 29.2 %copy-start.2 = (f32[128,128]{1,0:T(8,128)S(1)}, f32[128,128]{1,0:T(8,128)}, u32[]{:S(2)}) copy-start(f32[128,128]{1,0:T(8,128)} %refs_2_.3) | copy-start | bytes 196612
  0.7 29.2 %copy-start.3 = (f32[128,128]{1,0:T(8,128)S(1)}, f32[128,128]{1,0:T(8,128)}, u32[]{:S(2)}) copy-start(f32[128,128]{1,0:T(8,128)} %refs_3_.3) | copy-start | bytes 196612
  0.7 29.2 %copy-start.4 = (f32[128,128]{1,0:T(8,128)S(1)}, f32[128,128]{1,0:T(8,128)}, u32[]{:S(2)}) copy-start(f32[128,128]{1,0:T(8,128)} %refs_4_.3) | copy-start | bytes 196612
  0.7 29.2 %copy-start.5 = (f32[128,128]{1,0:T(8,128)S(1)}, f32[128,128]{1,0:T(8,128)}, u32[]{:S(2)}) copy-start(f32[128,128]{1,0:T(8,128)} %refs_5_.3) | copy-start | bytes 196612
  0.7 29.2 %copy-start.6 = (f32[128,128]{1,0:T(8,128)S(1)}, f32[128,128]{1,0:T(8,128)}, u32[]{:S(2)}) copy-start(f32[128,128]{1,0:T(8,128)} %refs_6_.3) | copy-start | bytes 196612
  0.7 29.2 %copy-start.7 = (f32[128,128]{1,0:T(8,128)S(1)}, f32[128,128]{1,0:T(8,128)}, u32[]{:S(2)}) copy-start(f32[128,128]{1,0:T(8,128)} %refs_7_.3) | copy-start | bytes 196612

commit v7 on v6

--- a/solution.py
+++ b/solution.py
@@ -232,7 +232,7 @@
     )
     ring_copies = lambda e: [
         remote(sent.at[e, 1], ring.at[e, k], ring_send.at[e, k], ring_recv.at[e, k], ring_at(k))
-        for k in range(1, pairs)
+        for k in (2, 1, 3)
     ]
     ends_copies = lambda: [
         remote(ends, ring_ends.at[k], ring_ends_send.at[k], ring_ends_recv.at[k], ring_at(k)) for k in range(1, pairs)

time: 32.6 us -> 32.6 us (level)
  no operation moved by 1% of the time
where the time goes in v7:
time: 32.6 us; the launch traced here: 32.4 us
  Pallas kernels  31.6 us (97%)
  between operations  0.77 us (2%)
    pallas_call x1, Pallas kernels, body(): pl.pallas_call(functools.partial(exchange, sides, faces), out_shape=(shap...  29.1 us
    pallas_call x1, Pallas kernels, body(): pl.pallas_call(functools.partial(substeps, sides), out_shape=(tile, tile,...  2.53 us

profile of v7, /device:TPU:1, one launch (start us, length us, event | category | flops | bytes accessed | tf_op | source)
XLA Modules:
  0.0 32.4 jit_solution(7288841701556627494)
XLA Ops:
  0.6 0.0 copy-start
  0.6 0.0 copy-start.1
  0.7 0.0 copy-start.2
  0.7 0.0 copy-start.3
  0.7 0.0 copy-start.4
  0.7 0.0 copy-start.5
  0.7 0.0 copy-start.6
  0.7 0.0 copy-start.7
  0.7 29.1 %shard_map.129 = (f32[4,16,128]{2,1,0:T(8,128)S(1)}, f32[16,128]{1,0:T(8,128)S(1)}) custom-call(s32[3,4,8]{2,1,0:T(4,128)} %bitcast.1, f32[8]{0:T(128)} %ph_ref.1, f32[128,128]{1,0:T(8,128)} %refs_0_.3, f32[128,128]{1,0:T(8,128)} %refs_1_.3, f32[128,128]{1,0:T(8,128)} %refs_2_.3, f32[128,128]{1,0:T(8,128)} %refs_3_.3, f32[128,128]{1,0:T(8,128)} %refs_4_.3, ...), custom_call_target="tpu_custom_call" | custom-call | tf_op jit(solution)/shard_map/pallas_call | solution.py:654
  29.8 0.0 copy-done
  29.8 0.0 copy-done.1
  29.8 0.0 copy-done.2
  29.8 0.0 copy-done.3
  29.8 0.0 copy-done.4
  29.8 0.0 copy-done.5
  29.8 0.0 copy-done.6
  29.8 0.0 copy-done.7
  29.9 2.5 %shard_map.130 = (f32[128,128]{1,0:T(8,128)}, f32[128,128]{1,0:T(8,128)}, f32[128,128]{1,0:T(8,128)}, f32[16,128,128]{2,1,0:T(8,128)}) custom-call(f32[4,16,128]{2,1,0:T(8,128)S(1)} %get-tuple-element.6.picked, f32[16,128]{1,0:T(8,128)S(1)} %get-tuple-element.7.coef, f32[128,128]{1,0:T(8,128)S(1)} %copy-done, f32[128,128]{1,0:T(8,128)S(1)} %copy-done.1, ...), custom_call_target="tpu_custom_call" | custom-call | tf_op jit(solution)/shard_map/pallas_call | solution.py:680
Async XLA Ops:
  0.6 29.1 %copy-start = (f32[128,128]{1,0:T(8,128)S(1)}, f32[128,128]{1,0:T(8,128)}, u32[]{:S(2)}) copy-start(f32[128,128]{1,0:T(8,128)} %refs_0_.3) | copy-start | bytes 196612
  0.6 29.1 %copy-start.1 = (f32[128,128]{1,0:T(8,128)S(1)}, f32[128,128]{1,0:T(8,128)}, u32[]{:S(2)}) copy-start(f32[128,128]{1,0:T(8,128)} %refs_1_.3) | copy-start | bytes 196612
  0.7 29.1 %copy-start.2 = (f32[128,128]{1,0:T(8,128)S(1)}, f32[128,128]{1,0:T(8,128)}, u32[]{:S(2)}) copy-start(f32[128,128]{1,0:T(8,128)} %refs_2_.3) | copy-start | bytes 196612
  0.7 29.1 %copy-start.3 = (f32[128,128]{1,0:T(8,128)S(1)}, f32[128,128]{1,0:T(8,128)}, u32[]{:S(2)}) copy-start(f32[128,128]{1,0:T(8,128)} %refs_3_.3) | copy-start | bytes 196612
  0.7 29.1 %copy-start.4 = (f32[128,128]{1,0:T(8,128)S(1)}, f32[128,128]{1,0:T(8,128)}, u32[]{:S(2)}) copy-start(f32[128,128]{1,0:T(8,128)} %refs_4_.3) | copy-start | bytes 196612
  0.7 29.1 %copy-start.5 = (f32[128,128]{1,0:T(8,128)S(1)}, f32[128,128]{1,0:T(8,128)}, u32[]{:S(2)}) copy-start(f32[128,128]{1,0:T(8,128)} %refs_5_.3) | copy-start | bytes 196612
  0.7 29.1 %copy-start.6 = (f32[128,128]{1,0:T(8,128)S(1)}, f32[128,128]{1,0:T(8,128)}, u32[]{:S(2)}) copy-start(f32[128,128]{1,0:T(8,128)} %refs_6_.3) | copy-start | bytes 196612
  0.7 29.1 %copy-start.7 = (f32[128,128]{1,0:T(8,128)S(1)}, f32[128,128]{1,0:T(8,128)}, u32[]{:S(2)}) copy-start(f32[128,128]{1,0:T(8,128)} %refs_7_.3) | copy-start | bytes 196612
